TPU v7x, 768 devices: a whole 4x8x12 slice. The times are simulated.
768 devices in a mesh: section: 64 (over y, z_hi, x), dp: 12 (over z_lo, core).
Axes of the slice: x: 4, y: 8, z: 12 (z_hi: 2, z_lo: 6; z = z_hi * 6 + z_lo), core: 2. Of those that a mesh axis runs over, the one named last changes fastest.
Arguments:
- stash_q: bfloat16 [64, 12, 128, 4096], P('section', 'dp'), may hold values from -5.5 to 5.5
- stash_kv: bfloat16 [64, 12, 128, 1024], P('section', 'dp'), may hold values from -5.5 to 5.5
- upstream: bfloat16 [64, 12, 128, 4096], P('section', 'dp'), may hold values from -6 to 6
- lengths: int32 [12], P('dp'), may hold values from 2 to 128, as said below
- domains: int32 [12], P('dp'), may hold values from 0 to 6
- domain_weight: float32 [7], replicated, may hold values from 0.3 to 3
Outputs:
- grad_q: bfloat16 [64, 12, 128, 4096], P('section', 'dp')
- grad_kv: bfloat16 [64, 12, 128, 1024], P('section', 'dp')
Inputs may be any that keep to these rules, and one draw needn't show every extreme that they name: `lengths`: some micro-batch has exactly 128 live tokens.
All inputs are finite; a program needn't handle non-finite values.
Results may differ from a plain program's by a relative error of at most 0.006.
Values may be sent and summed in bfloat16 or wider, within the bound.
No kernel may reach another device: no remote copies, remote signals or barrier semaphores. Data moves between devices by JAX's collectives and lax.ppermute only.
A program may use at most 32 MiB of HBM per device.

v0:
```python
import math

import jax
import jax.numpy as jnp
from jax import lax
from jax.sharding import PartitionSpec as P

QUERY_HEADS = 32
KEY_VALUE_HEADS = 4
HEAD_SIZE = 128
DOMAINS = 7


def shifted(array, axis, by):
    count = lax.axis_size(axis)
    return lax.ppermute(array, axis, [(i, (i + by) % count) for i in range(count)])


def swapped(array, axis, apart):
    return lax.ppermute(array, axis, [(i, i ^ 1 << apart) for i in range(lax.axis_size(axis))])


def backward_heads(query_rows, key_portion, value_portion, grads, lengths, kv_heads):
    batch_list = query_rows.shape[0]
    seq_len = query_rows.shape[1]
    head_dim = key_portion.shape[-1] // kv_heads
    group_count = query_rows.shape[-1] // (kv_heads * head_dim)
    inv_root = 1.0 / math.sqrt(head_dim)
    query_head_rows = query_rows.reshape(batch_list, seq_len, kv_heads, group_count, head_dim)
    key_head_rows = key_portion.reshape(batch_list, seq_len, kv_heads, head_dim)
    value_head_rows = value_portion.reshape(batch_list, seq_len, kv_heads, head_dim)
    row_index = jnp.arange(seq_len, dtype=jnp.int32)[:, None]
    col_index = jnp.arange(seq_len, dtype=jnp.int32)[None, :]
    allowed = (col_index <= row_index)[None] & (col_index[None] < lengths[:, None, None])
    live = jnp.arange(seq_len, dtype=jnp.int32)[None, :] < lengths[:, None]
    grad_masked = jnp.where(live[:, :, None], grads, jnp.zeros((), grads.dtype))
    gradient_heads = grad_masked.reshape(batch_list, seq_len, kv_heads, group_count, head_dim)
    scores = (
        jnp.einsum(
            "bikgd,bjkd->bkgij", query_head_rows, key_head_rows, preferred_element_type=jnp.float32
        )
        * inv_root
    )
    scores = jnp.where(allowed[:, None, None], scores, jnp.float32(-1e30))
    peak = jnp.max(scores, axis=-1, keepdims=True)
    expo = jnp.exp(scores - peak)
    probability = expo / jnp.sum(expo, axis=-1, keepdims=True)
    prob_half = probability.astype(jnp.bfloat16)
    value_gradient = jnp.einsum(
        "bkgij,bikgd->bjkd", prob_half, gradient_heads, preferred_element_type=jnp.float32
    )
    prob_grad = jnp.einsum(
        "bikgd,bjkd->bkgij", gradient_heads, value_head_rows, preferred_element_type=jnp.float32
    )
    row_total = jnp.sum(probability * prob_grad, axis=-1, keepdims=True)
    score_grad = (probability * (prob_grad - row_total) * inv_root).astype(jnp.bfloat16)
    query_grad = jnp.einsum(
        "bkgij,bjkd->bikgd", score_grad, key_head_rows, preferred_element_type=jnp.float32
    )
    key_gradient = jnp.einsum(
        "bkgij,bikgd->bjkd", score_grad, query_head_rows, preferred_element_type=jnp.float32
    )
    return (
        query_grad.reshape(batch_list, seq_len, kv_heads * group_count * head_dim),
        key_gradient.reshape(batch_list, seq_len, kv_heads * head_dim),
        value_gradient.reshape(batch_list, seq_len, kv_heads * head_dim),
    )


def body(stash_q, stash_kv, upstream, lengths, domains, domain_weight):
    section_bits = lax.axis_size("section").bit_length() - 1
    domain_ids = jnp.arange(DOMAINS, dtype=jnp.int32)
    onehot = domains[:, None] == domain_ids[None, :]
    partial_count = jnp.sum(jnp.where(onehot, lengths[:, None], 0), axis=0)
    counts = lax.psum(partial_count, "dp").astype(jnp.float32)
    token_total = jnp.sum(counts)
    own_count = jnp.sum(jnp.where(onehot, counts[None, :], jnp.float32(0.0)), axis=1)
    weight = jnp.sum(jnp.where(onehot, domain_weight[None, :], jnp.float32(0.0)), axis=1)
    factor = weight * token_total / (DOMAINS * own_count)
    next_grads = shifted(upstream, "section", -1)[0]
    key_span = KEY_VALUE_HEADS * HEAD_SIZE
    group_span = QUERY_HEADS // KEY_VALUE_HEADS * HEAD_SIZE
    query_list = []
    key_list = []
    value_list = []
    query_got, pair_got = swapped((stash_q, stash_kv), "section", section_bits - 1)
    query_all = query_got[0]
    pair_all = pair_got[0]
    for head_number in range(KEY_VALUE_HEADS):
        query_part = query_all[..., head_number * group_span : (head_number + 1) * group_span]
        key_part = pair_all[..., head_number * HEAD_SIZE : (head_number + 1) * HEAD_SIZE]
        value_part = pair_all[
            ..., key_span + head_number * HEAD_SIZE : key_span + (head_number + 1) * HEAD_SIZE
        ]
        grad_part = next_grads[..., head_number * group_span : (head_number + 1) * group_span]
        query_grad, key_gradient, value_gradient = backward_heads(
            query_part, key_part, value_part, grad_part, lengths, 1
        )
        query_list.append(query_grad)
        key_list.append(key_gradient)
        value_list.append(value_gradient)
    query_grad = jnp.concatenate(query_list, axis=-1)
    key_gradient = jnp.concatenate(key_list, axis=-1)
    value_gradient = jnp.concatenate(value_list, axis=-1)
    row_scales = factor[:, None, None]
    out_q = (query_grad * row_scales).astype(jnp.bfloat16)
    out_kv = jnp.concatenate(
        [key_gradient * row_scales, value_gradient * row_scales], axis=-1
    ).astype(jnp.bfloat16)
    return (out_q[None], out_kv[None])


def solution(mesh):
    return jax.shard_map(
        body,
        mesh=mesh,
        in_specs=(
            P("section", "dp", None, None),
            P("section", "dp", None, None),
            P("section", "dp", None, None),
            P("dp"),
            P("dp"),
            P(),
        ),
        out_specs=(P("section", "dp", None, None), P("section", "dp", None, None)),
        check_vma=False,
    )
```

profile of v0, /device:TPU:32, one launch (start us, length us, event | category | flops | bytes accessed | tf_op | source)
XLA Modules:
  0.0 142.7 jit_solution(15160981129767006314)
XLA Ops:
  0.6 17.2 %collective-permute-start.2 = (bf16[1,1,128,4096]{3,2,1,0:T(8,128)(2,1)}, bf16[1,1,128,4096]{3,2,1,0:T(8,128)(2,1)S(1)}, u32[]{:S(2)}, u32[]{:S(2)}) collective-permute-start(bf16[1,1,128,4096]{3,2,1,0:T(8,128)(2,1)} %param.8), channel_id=1, source_target_pairs={{0,756},{12,0},{24,12},{36,24},{48,36},{60,48},{72,60},{84,72},{96... | collective-permute-start | bytes 3145736 | tf_op jit(solution)/shard_map/ppermute | solution.py:16
  17.9 1.6 %copy.41 = bf16[1,1,128,4096]{2,3,1,0:T(8,128)(2,1)S(1)} copy(bf16[1,1,128,4096]{3,2,1,0:T(8,128)(2,1)} %param.6) | data formatting | bytes 2097152 | tf_op args[0]
  19.5 5.0 %collective-permute-start.1 = (bf16[1,1,128,4096]{2,3,1,0:T(8,128)(2,1)S(1)}, bf16[1,1,128,4096]{2,3,1,0:T(8,128)(2,1)S(1)}, u32[]{:S(2)}, u32[]{:S(2)}) collective-permute-start(bf16[1,1,128,4096]{2,3,1,0:T(8,128)(2,1)S(1)} %copy.41), channel_id=1, source_target_pairs={{0,384},{12,396},{24,408},{36,420},{48,432},{60,444},{72,456},{84,... | collective-permute-start | bytes 3145736 | tf_op jit(solution)/shard_map/ppermute | solution.py:20
  25.8 4.7 %collective-permute-start = (bf16[1,1,128,1024]{3,2,1,0:T(8,128)(2,1)}, bf16[1,1,128,1024]{3,2,1,0:T(8,128)(2,1)S(1)}, u32[]{:S(2)}, u32[]{:S(2)}) collective-permute-start(bf16[1,1,128,1024]{3,2,1,0:T(8,128)(2,1)} %param.7), channel_id=1, source_target_pairs={{0,384},{12,396},{24,408},{36,420},{48,432},{60,444},{72,456},{84,... | collective-permute-start | bytes 786440 | tf_op jit(solution)/shard_map/ppermute | solution.py:20
  30.6 92.6 %psum.7 = s32[7]{0:T(128)S(1)} all-reduce(s32[7]{0:T(128)S(1)} %fusion.38), channel_id=1, replica_groups=mesh['section'=64,'dp'=12] {'dp'}, use_global_device_ids=true, to_apply=%region_13.14 | all-reduce | flops 7 | bytes 56 | tf_op jit(solution)/shard_map/psum | solution.py:75
  123.1 0.7 select_reduce_fusion.1
  123.8 0.6 select_reduce_fusion
  126.8 0.2 fusion.43
  127.1 0.2 multiply_reduce_fusion.3
  127.6 0.2 convolution_bitcast_fusion.11
  127.8 0.3 fusion.34
  128.1 0.2 fusion.42
  128.5 0.2 multiply_reduce_fusion.2
  128.7 0.3 copy-done.1
  129.3 0.2 convolution_bitcast_fusion.10
  129.5 0.3 fusion.35
  129.8 0.2 fusion.41
  130.2 0.2 multiply_reduce_fusion.1
  130.4 0.3 copy-done.3
  130.9 0.9 convolution_bitcast_fusion.9
  131.8 0.3 fusion.36
  132.5 0.2 multiply_reduce_fusion
  132.7 0.3 copy-done.5
  133.2 0.9 convolution_bitcast_fusion.8
  134.1 0.3 fusion.37
  134.6 1.9 %convolution_bitcast_fusion.7 = f32[128,128]{0,1:T(8,128)} fusion(bf16[128,8,128]{2,1,0:T(8,128)(2,1)} %bitcast.309, bf16[8,128,128]{2,0,1:T(8,128)(2,1)S(1)} %copy.92), kind=kOutput, calls=%fused_computation.21 | convolution fusion | flops 33554432 | bytes 589824 | tf_op jit(solution)/shard_map/bkgij,bikgd->bjkd/dot_general | solution.py:49
  136.7 0.9 convolution_bitcast_fusion.6
  137.8 0.9 convolution_bitcast_fusion.5
  138.9 0.3 convolution_bitcast_fusion.4
  139.2 0.5 copy-done.7
  139.9 0.9 copy.74
  141.6 1.1 fusion
  (53 shorter events, 3.6 us)
Async XLA Ops:
  0.6 122.5 %copy-start.12 = (f32[7]{0:T(128)S(1)}, f32[7]{0:T(128)}, u32[]{:S(2)}) copy-start(f32[7]{0:T(128)} %param.11) | copy-start | bytes 88
  0.6 125.8 %collective-permute-start.2 = (bf16[1,1,128,4096]{3,2,1,0:T(8,128)(2,1)}, bf16[1,1,128,4096]{3,2,1,0:T(8,128)(2,1)S(1)}, u32[]{:S(2)}, u32[]{:S(2)}) collective-permute-start(bf16[1,1,128,4096]{3,2,1,0:T(8,128)(2,1)} %param.8), channel_id=1, source_target_pairs={{0,756},{12,0},{24,12},{36,24},{48,36},{60,48},{72,60},{84,72},{96... | collective-permute-start | bytes 3145736 | tf_op jit(solution)/shard_map/ppermute | solution.py:16
  19.5 107.2 %collective-permute-start.1 = (bf16[1,1,128,4096]{2,3,1,0:T(8,128)(2,1)S(1)}, bf16[1,1,128,4096]{2,3,1,0:T(8,128)(2,1)S(1)}, u32[]{:S(2)}, u32[]{:S(2)}) collective-permute-start(bf16[1,1,128,4096]{2,3,1,0:T(8,128)(2,1)S(1)} %copy.41), channel_id=1, source_target_pairs={{0,384},{12,396},{24,408},{36,420},{48,432},{60,444},{72,456},{84,... | collective-permute-start | bytes 3145736 | tf_op jit(solution)/shard_map/ppermute | solution.py:20
  25.8 100.9 %collective-permute-start = (bf16[1,1,128,1024]{3,2,1,0:T(8,128)(2,1)}, bf16[1,1,128,1024]{3,2,1,0:T(8,128)(2,1)S(1)}, u32[]{:S(2)}, u32[]{:S(2)}) collective-permute-start(bf16[1,1,128,1024]{3,2,1,0:T(8,128)(2,1)} %param.7), channel_id=1, source_target_pairs={{0,384},{12,396},{24,408},{36,420},{48,432},{60,444},{72,456},{84,... | collective-permute-start | bytes 786440 | tf_op jit(solution)/shard_map/ppermute | solution.py:20
  126.7 0.7 copy-start
  128.4 0.7 copy-start.1
  130.0 0.7 copy-start.3
  132.3 0.7 copy-start.5
  134.6 2.1 %copy-start.2 = (bf16[16,8,8,128]{3,2,1,0:T(8,128)(2,1)S(1)}, bf16[16,8,8,128]{3,2,1,0:T(8,128)(2,1)}, u32[]{:S(2)}) copy-start(bf16[16,8,8,128]{3,2,1,0:T(8,128)(2,1)} %copy-done.1) | copy-start | bytes 786436
  136.7 1.1 copy-start.4
  137.8 1.1 copy-start.6
  138.9 0.8 copy-start.7
  138.9 0.9 copy-start.8
  138.9 0.9 copy-start.9
  138.9 0.9 copy-start.10
  138.9 0.9 copy-start.11
where the time goes:
time: 143 us
  blocking collectives  92.6 us (65%)
  starting transfers between devices  27 us (19%)
  matrix products  9.05 us (6%)
  local copies, waits for them, and re-layouts  5.99 us (4%)
  between operations  4.35 us (3%)
  other arithmetic  3.8 us (3%)
    psum x1, blocking collectives, body(): counts = lax.psum(partial_count, 'dp').astype(jnp.float32)  92.6 us
    ppermute x1, starting transfers between devices, shifted(): lax.ppermute(array, axis, [(i, (i + by) % count) for i in range(count)])  17.2 us
    ppermute x2, starting transfers between devices, swapped(): lax.ppermute(array, axis, [(i, i ^ 1 << apart) for i in range(lax.axis_si...  9.75 us
    unnamed x32, local copies, waits for them, and re-layouts  4.38 us
    dot_general x4, matrix products, backward_heads(): jnp.einsum('bkgij,bikgd->bjkd', prob_half, gradient_heads, preferred_elem...  3.97 us
  transfers between devices with their start and end apart: 3, of which 0 were waited for; matrix products, arithmetic and copies ran while one was open for 2% of the time, Pallas kernels for 0%

commit v1 on v0

v1 whole, which is shorter than its diff:
```python
import functools
import math

import jax
import jax.numpy as jnp
from jax import lax
from jax.experimental import pallas as pl
from jax.experimental.pallas import tpu as pltpu
from jax.sharding import PartitionSpec as P

KV_HEADS = 4
GROUP = 8
HEAD = 128
DOMAINS = 7
TOKENS = 128
REPLICAS = 12
NY, NZ, NX = 8, 2, 4

INV_ROOT = 1.0 / math.sqrt(HEAD)
LOG_SCALE = INV_ROOT * math.log2(math.e)
NT = (((1,), (1,)), ((), ()))
TN = (((0,), (0,)), ((), ()))


def section_pairs(move):
    pairs = []
    for y in range(NY):
        for z in range(NZ):
            for x in range(NX):
                to = move(y, z, x)
                if to is not None:
                    ty, tz, tx = to
                    pairs.append(((y * NZ + z) * NX + x, ((ty % NY) * NZ + tz % NZ) * NX + tx % NX))
    return pairs


def moved(array, move):
    return lax.ppermute(array, "section", section_pairs(move))


def opposite(y, z, x):
    return y + 4, z, x


def previous(y, z, x):
    return (y, z, x - 1) if x else (y - 1 + z, z + 1, 3)


def x_ring(y, z, x):
    return y, z, x - 1


def facts_of(facts_ref):
    number = lambda value: value.astype(jnp.int32)
    own = number(facts_ref[0, 3])
    domain = facts_ref[own, 1]
    total = jnp.float32(0)
    count = jnp.float32(0)
    for b in range(REPLICAS):
        n = facts_ref[b, 0]
        total += n
        count += jnp.where(facts_ref[b, 1] == domain, n, jnp.float32(0))
    weight = jnp.full((1, HEAD), facts_ref[0, 4 + number(domain)], jnp.float32)
    total = jnp.full((1, HEAD), total, jnp.float32)
    count = jnp.full((1, HEAD), count, jnp.float32)
    return number(facts_ref[own, 0]), number(facts_ref[0, 2]) == NX - 1, weight * total / (DOMAINS * count)


def one_group(live_tokens, factor, query, key, value, grad):
    width = GROUP * TOKENS
    j = lax.broadcasted_iota(jnp.int32, (TOKENS, width), 0)
    i = lax.broadcasted_iota(jnp.int32, (TOKENS, width), 1) % TOKENS
    allowed = (j <= i) & (j < live_tokens)
    live = (lax.broadcasted_iota(jnp.int32, (1, width), 1) % TOKENS) < live_tokens
    scores = lax.dot_general(key, query, NT, preferred_element_type=jnp.float32)
    prob_grad = lax.dot_general(value, grad, NT, preferred_element_type=jnp.float32)
    scores = jnp.where(allowed, scores, jnp.float32(-1e30))
    peak = jnp.max(scores, axis=0, keepdims=True)
    expo = jnp.exp2((scores - peak) * LOG_SCALE)
    share = jnp.where(live, 1.0 / jnp.sum(expo, axis=0, keepdims=True), 0.0)
    prob = expo * share
    value_grad = jnp.dot(prob.astype(jnp.bfloat16), grad, preferred_element_type=jnp.float32)
    row_total = jnp.sum(prob * prob_grad, axis=0, keepdims=True)
    score_grad = (prob * (prob_grad - row_total) * INV_ROOT).astype(jnp.bfloat16)
    key_grad = jnp.dot(score_grad, query, preferred_element_type=jnp.float32)
    query_grad = lax.dot_general(score_grad, key, TN, preferred_element_type=jnp.float32)
    return (
        (query_grad * factor).astype(jnp.bfloat16),
        (key_grad * factor).astype(jnp.bfloat16),
        (value_grad * factor).astype(jnp.bfloat16),
    )


def kernel(groups, parts, *refs):
    facts_ref, q_ref, kv_ref = refs[:3]
    grads = refs[3:-5]
    out_q, out_kv, dq, dkv, sem = refs[-5:]
    live_tokens, far, factor = facts_of(facts_ref)
    copies = []
    for at, group in enumerate(groups):
        queries, gradients = [], []
        for head in range(at * GROUP, (at + 1) * GROUP):
            queries.append(q_ref[:, head * HEAD : (head + 1) * HEAD])
            plain, other, column, other_column = parts[head]
            g = grads[plain][:, column : column + HEAD]
            if other is not None:
                g = jnp.where(far, grads[other][:, other_column : other_column + HEAD], g)
            gradients.append(g)
        key = kv_ref[:, group * HEAD : (group + 1) * HEAD]
        value = kv_ref[:, (KV_HEADS + group) * HEAD : (KV_HEADS + group + 1) * HEAD]
        query_grad, key_grad, value_grad = one_group(
            live_tokens, factor, jnp.concatenate(queries, 0), key, value, jnp.concatenate(gradients, 0)
        )
        for t in range(GROUP):
            dq[at, :, t * HEAD : (t + 1) * HEAD] = query_grad[t * TOKENS : (t + 1) * TOKENS]
        dkv[2 * at] = key_grad
        dkv[2 * at + 1] = value_grad
        span = GROUP * HEAD
        for n, (src, dst) in enumerate(
            (
                (dq.at[at], out_q.at[:, group * span : (group + 1) * span]),
                (dkv.at[2 * at], out_kv.at[:, group * HEAD : (group + 1) * HEAD]),
                (dkv.at[2 * at + 1], out_kv.at[:, (KV_HEADS + group) * HEAD : (KV_HEADS + group + 1) * HEAD]),
            )
        ):
            copy = pltpu.make_async_copy(src, dst, sem.at[3 * at + n])
            copy.start()
            copies.append(copy)
    for copy in copies:
        copy.wait()


def attend(groups, parts, facts, arrays, outputs=()):
    vmem = pl.BlockSpec(memory_space=pltpu.VMEM)
    smem = pl.BlockSpec(memory_space=pltpu.SMEM)
    hbm = pl.BlockSpec(memory_space=pl.ANY)
    count = len(groups)
    operands = (facts, *arrays, *outputs)
    first = 1 + len(arrays)
    elements = count * GROUP * TOKENS * HEAD
    return pl.pallas_call(
        functools.partial(kernel, groups, parts),
        out_shape=(
            jax.ShapeDtypeStruct((TOKENS, KV_HEADS * GROUP * HEAD), jnp.bfloat16),
            jax.ShapeDtypeStruct((TOKENS, 2 * KV_HEADS * HEAD), jnp.bfloat16),
        ),
        in_specs=[smem] + [vmem] * len(arrays) + [hbm] * len(outputs),
        out_specs=(hbm, hbm),
        scratch_shapes=[
            pltpu.VMEM((count, TOKENS, GROUP * HEAD), jnp.bfloat16),
            pltpu.VMEM((2 * count, TOKENS, HEAD), jnp.bfloat16),
            pltpu.SemaphoreType.DMA((3 * count,)),
        ],
        input_output_aliases={first + i: i for i in range(len(outputs))},
        compiler_params=pltpu.CompilerParams(vmem_limit_bytes=24 << 20),
        cost_estimate=pl.CostEstimate(flops=10 * elements * TOKENS, bytes_accessed=6 * elements, transcendentals=elements),
    )(*operands)


def across(column):
    return lambda y, z, x: (y - 1 + z, z + 1, 3) if x == column else None


def body(stash_q, stash_kv, upstream, lengths, domains, domain_weight):
    x = lax.axis_index("section") % NX
    span = GROUP * HEAD
    kv = moved(stash_kv, opposite)
    q_most = moved(stash_q[..., : 3 * span], opposite)
    q_last = moved(stash_q[..., 3 * span :], opposite)
    part = lambda first, count: upstream[..., first * span : (first + count) * span]
    b_near = moved(part(1, 1), x_ring)
    c_mid = moved(part(2, 1), lambda y, z, x: (y, z, 1) if x == 0 else None)
    d_mid = moved(part(3, 1), lambda y, z, x: (y, z, 2) if x == 0 else None)
    cd_near = moved(part(2, 2), lambda y, z, x: (y, z, x - 1) if x else None)
    a_all = moved(part(0, 1), previous)
    b_far = moved(b_near, across(3))
    c_far = moved(c_mid, across(1))
    d_far = moved(d_mid, across(2))
    own = jnp.concatenate([lengths, domains, x[None]]).astype(jnp.float32)
    to = jnp.arange(REPLICAS, dtype=jnp.float32)[:, None]
    row = lambda v: jnp.broadcast_to(v[None], (REPLICAS, v.shape[0]))
    facts = jnp.concatenate([row(own), to, row(domain_weight)], axis=1)
    facts = lax.all_to_all(facts, "dp", 0, 0, tiled=True)
    flat = lambda a: a.reshape(a.shape[2:])
    column = lambda h: (h % GROUP) * HEAD
    parts = [(0, None, column(h), 0) for h in range(8)]
    parts += [(1, 3, column(h), column(h)) for h in range(8)]
    parts += [(2, 4, column(h), column(h)) for h in range(8)]
    last = [(0, 1, column(h) + span, column(h)) for h in range(8)]
    arrays = (q_most, kv, a_all, b_near, cd_near, b_far, c_far)
    outs = attend((0, 1, 2), parts, facts, [flat(a) for a in arrays])
    arrays = (q_last, kv, cd_near, d_far)
    out_q, out_kv = attend((3,), last, facts, [flat(a) for a in arrays], outs)
    return out_q[None, None], out_kv[None, None]


def solution(mesh):
    spec = P("section", "dp", None, None)
    return jax.shard_map(
        body,
        mesh=mesh,
        in_specs=(spec, spec, spec, P("dp"), P("dp"), P()),
        out_specs=(spec, spec),
        check_vma=False,
    )
```

time: 143 us -> 117 us (0.82)
  the two profiles are of different devices: /device:TPU:32 before, /device:TPU:36 now
where the time goes in v1:
time: 117 us
  starting transfers between devices  49.5 us (42%)
  waiting for transfers between devices  28.3 us (24%)
  blocking collectives  26.8 us (23%)
  Pallas kernels  5.49 us (5%)
  local copies, waits for them, and re-layouts  4.6 us (4%)
  between operations  2.16 us (2%)
    ppermute x11, starting transfers between devices, moved(): return lax.ppermute(array, 'section', section_pairs(move))  49.5 us
    ppermute x11, waiting for transfers between devices, moved(): return lax.ppermute(array, 'section', section_pairs(move))  28.3 us
    all_to_all x1, blocking collectives, body(): facts = lax.all_to_all(facts, 'dp', 0, 0, tiled=True)  26.8 us
    pallas_call x2, Pallas kernels, attend(): pl.pallas_call(functools.partial(kernel, groups, parts), out_shape=(jax.S...  5.49 us
    slice x2, local copies, waits for them, and re-layouts, body(): upstream[..., first * span:(first + count) * span]  2.89 us
  transfers between devices with their start and end apart: 11, of which 1 were waited for; matrix products, arithmetic and copies ran while one was open for 2% of the time, Pallas kernels for 3%

profile of v1, /device:TPU:36, one launch (start us, length us, event | category | flops | bytes accessed | tf_op | source)
XLA Modules:
  0.0 117.0 jit_solution(14909902067717245971)
XLA Ops:
  0.6 2.1 %fusion = (bf16[1,1,128,1024]{3,2,1,0:T(8,128)(2,1)S(1)}, bf16[1,1,128,1024]{3,2,1,0:T(8,128)(2,1)S(1)}, bf16[1,1,128,1024]{3,2,1,0:T(8,128)(2,1)}, bf16[1,1,128,1024]{3,2,1,0:T(8,128)(2,1)S(1)}) fusion(bf16[1,1,128,4096]{3,2,1,0:T(8,128)(2,1)} %param.8), kind=kLoop, calls=%fused_computation.3 | loop fusion | bytes 2097152 | tf_op jit(solution)/shard_map/slice | solution.py:170
  2.7 2.6 %collective-permute-start.7 = (bf16[1,1,128,1024]{3,2,1,0:T(8,128)(2,1)S(1)}, bf16[1,1,128,1024]{3,2,1,0:T(8,128)(2,1)S(1)}, u32[]{:S(2)}, u32[]{:S(2)}) collective-permute-start(bf16[1,1,128,1024]{3,2,1,0:T(8,128)(2,1)S(1)} %get-tuple-element.13), channel_id=1, source_target_pairs={{0,36},{12,0},{24,12},{36,24},{48,84},{60,48},{72,60},{84,72},{96,... | collective-permute-start | bytes 786440 | tf_op jit(solution)/shard_map/ppermute | solution.py:38
  5.3 0.9 slice.24
  6.2 2.0 %collective-permute-start.5 = (bf16[1,1,128,3072]{3,2,1,0:T(8,128)(2,1)}, bf16[1,1,128,3072]{3,2,1,0:T(8,128)(2,1)S(1)}, u32[]{:S(2)}, u32[]{:S(2)}) collective-permute-start(bf16[1,1,128,3072]{3,2,1,0:T(8,128)(2,1)} %slice.24), channel_id=1, source_target_pairs={{0,384},{12,396},{24,408},{36,420},{48,432},{60,444},{72,456},{84,... | collective-permute-start | bytes 2359304 | tf_op jit(solution)/shard_map/ppermute | solution.py:38
  8.2 0.7 collective-permute-start.9
  8.9 12.0 %collective-permute-start.6 = (bf16[1,1,128,1024]{3,2,1,0:T(8,128)(2,1)S(1)}, bf16[1,1,128,1024]{3,2,1,0:T(8,128)(2,1)S(1)}, u32[]{:S(2)}, u32[]{:S(2)}) collective-permute-start(bf16[1,1,128,1024]{3,2,1,0:T(8,128)(2,1)S(1)} %get-tuple-element.11), channel_id=1, source_target_pairs={{0,756},{12,0},{24,12},{36,24},{48,36},{60,48},{72,60},{84,72},{96... | collective-permute-start | bytes 786440 | tf_op jit(solution)/shard_map/ppermute | solution.py:38
  21.0 1.9 %collective-permute-start.1 = (bf16[1,1,128,1024]{3,2,1,0:T(8,128)(2,1)}, bf16[1,1,128,1024]{3,2,1,0:T(8,128)(2,1)S(1)}, u32[]{:S(2)}, u32[]{:S(2)}) collective-permute-start(bf16[1,1,128,1024]{3,2,1,0:T(8,128)(2,1)} %param.7), channel_id=1, source_target_pairs={{0,384},{12,396},{24,408},{36,420},{48,432},{60,444},{72,456},{84,... | collective-permute-start | bytes 786440 | tf_op jit(solution)/shard_map/ppermute | solution.py:38
  22.9 0.8 slice.22
  23.7 0.0 collective-permute-done.7
  23.7 4.6 %collective-permute-start.2 = (bf16[1,1,128,2048]{3,2,1,0:T(8,128)(2,1)}, bf16[1,1,128,2048]{3,2,1,0:T(8,128)(2,1)S(1)}, u32[]{:S(2)}, u32[]{:S(2)}) collective-permute-start(bf16[1,1,128,2048]{3,2,1,0:T(8,128)(2,1)} %slice.22), channel_id=1, source_target_pairs={{12,0},{24,12},{36,24},{60,48},{72,60},{84,72},{108,96},{120,108},... | collective-permute-start | bytes 1572872 | tf_op jit(solution)/shard_map/ppermute | solution.py:38
  28.3 0.0 collective-permute-done.9
  28.3 1.3 %collective-permute-start.3 = (bf16[1,1,128,1024]{3,2,1,0:T(8,128)(2,1)}, bf16[1,1,128,1024]{3,2,1,0:T(8,128)(2,1)}, u32[]{:S(2)}, u32[]{:S(2)}) collective-permute-start(bf16[1,1,128,1024]{3,2,1,0:T(8,128)(2,1)} %get-tuple-element.12), channel_id=1, source_target_pairs={{0,24},{48,72},{96,120},{144,168},{192,216},{240,264},{288,312},{3... | collective-permute-start | bytes 786440 | tf_op jit(solution)/shard_map/ppermute | solution.py:38
  29.6 0.0 collective-permute-done.6
  29.6 0.7 collective-permute-start.8
  31.6 28.2 %collective-permute-done.1 = bf16[1,1,128,1024]{3,2,1,0:T(8,128)(2,1)S(1)} collective-permute-done((bf16[1,1,128,1024]{3,2,1,0:T(8,128)(2,1)}, bf16[1,1,128,1024]{3,2,1,0:T(8,128)(2,1)S(1)}, u32[]{:S(2)}, u32[]{:S(2)}) %collective-permute-start.1) | collective-permute-done | bytes 262176 | tf_op jit(solution)/shard_map/ppermute | solution.py:38
  59.9 0.7 collective-permute-start.10
  60.5 0.1 add_convert_fusion
  60.7 0.0 copy-start.3
  60.7 0.6 copy-done.3
  61.3 0.1 pad.2.clone
  61.4 0.0 collective-permute-done.3
  61.4 1.9 %collective-permute-start = (bf16[1,1,128,1024]{3,2,1,0:T(8,128)(2,1)S(1)}, bf16[1,1,128,1024]{3,2,1,0:T(8,128)(2,1)S(1)}, u32[]{:S(2)}, u32[]{:S(2)}) collective-permute-start(bf16[1,1,128,1024]{3,2,1,0:T(8,128)(2,1)S(1)} %slice.21), channel_id=1, source_target_pairs={{0,384},{12,396},{24,408},{36,420},{48,432},{60,444},{72,456},{84,... | collective-permute-start | bytes 786440 | tf_op jit(solution)/shard_map/ppermute | solution.py:38
  63.3 0.0 collective-permute-done.8
  63.3 21.2 %collective-permute-start.4 = (bf16[1,1,128,1024]{3,2,1,0:T(8,128)(2,1)}, bf16[1,1,128,1024]{3,2,1,0:T(8,128)(2,1)S(1)}, u32[]{:S(2)}, u32[]{:S(2)}) collective-permute-start(bf16[1,1,128,1024]{3,2,1,0:T(8,128)(2,1)} %collective-permute-done.3), channel_id=1, source_target_pairs={{24,756},{72,36},{120,84},{168,132},{216,180},{264,228},{312,276},... | collective-permute-start | bytes 786440 | tf_op jit(solution)/shard_map/ppermute | solution.py:38
  84.5 0.1 maximum_bitcast_fusion
  84.6 26.8 %all_to_all.11 = f32[12,1,11]{2,1,0:T(1,128)S(1)} all-to-all(f32[12,1,11]{2,1,0:T(1,128)S(1)} %copy.10), channel_id=1, replica_groups=mesh['section'=64,'dp'=12] {'dp'}, dimensions={0} | all-to-all | bytes 1056 | tf_op jit(solution)/shard_map/all_to_all | solution.py:183
  111.4 0.0 collective-permute-done.10
  111.4 0.0 collective-permute-done.2
  111.5 3.3 %shard_map.77 = (bf16[128,4096]{1,0:T(8,128)(2,1)}, bf16[128,1024]{1,0:T(8,128)(2,1)}) custom-call(f32[12,11]{1,0:T(8,128)S(1)} %bitcast.28, bf16[128,3072]{1,0:T(8,128)(2,1)S(1)} %bitcast.21, bf16[128,1024]{1,0:T(8,128)(2,1)S(1)} %bitcast.19, bf16[128,1024]{1,0:T(8,128)(2,1)S(1)} %bitcast.23, bf16[128,1024]{1,0:T(8,128)(2,1)S(1)} %bitcast.22, ...), custom_call_target="tpu_custom_call" | custom-call | flops 503316480 | bytes 2359296 | tf_op jit(solution)/shard_map/pallas_call | solution.py:141
  114.8 0.0 collective-permute-done
  114.8 0.0 collective-permute-done.4
  114.8 2.2 %shard_map.78 = (bf16[128,4096]{1,0:T(8,128)(2,1)}, bf16[128,1024]{1,0:T(8,128)(2,1)}) custom-call(f32[12,11]{1,0:T(8,128)S(1)} %bitcast.29, bf16[128,1024]{1,0:T(8,128)(2,1)S(1)} %bitcast.26, bf16[128,1024]{1,0:T(8,128)(2,1)S(1)} %bitcast.20, bf16[128,2048]{1,0:T(8,128)(2,1)S(1)} %bitcast.18, ...), custom_call_target="tpu_custom_call", output_to_operand_aliasing={{0}: (5, {}), {1}: (6, {})} | custom-call | flops 167772160 | bytes 786432 | tf_op jit(solution)/shard_map/pallas_call | solution.py:141
  (12 shorter events, 0.1 us)
Async XLA Ops:
  0.6 4.6 %copy-start.1 = (bf16[1,1,128,4096]{3,2,1,0:T(8,128)(2,1)S(1)}, bf16[1,1,128,4096]{3,2,1,0:T(8,128)(2,1)}, u32[]{:S(2)}) copy-start(bf16[1,1,128,4096]{3,2,1,0:T(8,128)(2,1)} %param.6) | copy-start | bytes 3145732
  2.7 20.2 %copy-start = (bf16[1,1,128,4096]{3,2,1,0:T(8,128)(2,1)S(1)}, bf16[1,1,128,4096]{3,2,1,0:T(8,128)(2,1)}, u32[]{:S(2)}) copy-start(bf16[1,1,128,4096]{3,2,1,0:T(8,128)(2,1)} %param.8) | copy-start | bytes 3145732
  2.7 21.1 %collective-permute-start.7 = (bf16[1,1,128,1024]{3,2,1,0:T(8,128)(2,1)S(1)}, bf16[1,1,128,1024]{3,2,1,0:T(8,128)(2,1)S(1)}, u32[]{:S(2)}, u32[]{:S(2)}) collective-permute-start(bf16[1,1,128,1024]{3,2,1,0:T(8,128)(2,1)S(1)} %get-tuple-element.13), channel_id=1, source_target_pairs={{0,36},{12,0},{24,12},{36,24},{48,84},{60,48},{72,60},{84,72},{96,... | collective-permute-start | bytes 786440 | tf_op jit(solution)/shard_map/ppermute | solution.py:38
  6.2 105.2 %collective-permute-start.5 = (bf16[1,1,128,3072]{3,2,1,0:T(8,128)(2,1)}, bf16[1,1,128,3072]{3,2,1,0:T(8,128)(2,1)S(1)}, u32[]{:S(2)}, u32[]{:S(2)}) collective-permute-start(bf16[1,1,128,3072]{3,2,1,0:T(8,128)(2,1)} %slice.24), channel_id=1, source_target_pairs={{0,384},{12,396},{24,408},{36,420},{48,432},{60,444},{72,456},{84,... | collective-permute-start | bytes 2359304 | tf_op jit(solution)/shard_map/ppermute | solution.py:38
  8.2 20.1 %collective-permute-start.9 = (bf16[1,1,128,1024]{3,2,1,0:T(8,128)(2,1)S(1)}, bf16[1,1,128,1024]{3,2,1,0:T(8,128)(2,1)S(1)}, u32[]{:S(2)}, u32[]{:S(2)}) collective-permute-start(bf16[1,1,128,1024]{3,2,1,0:T(8,128)(2,1)S(1)} %get-tuple-element.10), channel_id=1, source_target_pairs={{0,12},{48,60},{96,108},{144,156},{192,204},{240,252},{288,300},{3... | collective-permute-start | bytes 786440 | tf_op jit(solution)/shard_map/ppermute | solution.py:38
  8.9 20.7 %collective-permute-start.6 = (bf16[1,1,128,1024]{3,2,1,0:T(8,128)(2,1)S(1)}, bf16[1,1,128,1024]{3,2,1,0:T(8,128)(2,1)S(1)}, u32[]{:S(2)}, u32[]{:S(2)}) collective-permute-start(bf16[1,1,128,1024]{3,2,1,0:T(8,128)(2,1)S(1)} %get-tuple-element.11), channel_id=1, source_target_pairs={{0,756},{12,0},{24,12},{36,24},{48,36},{60,48},{72,60},{84,72},{96... | collective-permute-start | bytes 786440 | tf_op jit(solution)/shard_map/ppermute | solution.py:38
  21.0 38.9 %collective-permute-start.1 = (bf16[1,1,128,1024]{3,2,1,0:T(8,128)(2,1)}, bf16[1,1,128,1024]{3,2,1,0:T(8,128)(2,1)S(1)}, u32[]{:S(2)}, u32[]{:S(2)}) collective-permute-start(bf16[1,1,128,1024]{3,2,1,0:T(8,128)(2,1)} %param.7), channel_id=1, source_target_pairs={{0,384},{12,396},{24,408},{36,420},{48,432},{60,444},{72,456},{84,... | collective-permute-start | bytes 786440 | tf_op jit(solution)/shard_map/ppermute | solution.py:38
  23.7 87.7 %collective-permute-start.2 = (bf16[1,1,128,2048]{3,2,1,0:T(8,128)(2,1)}, bf16[1,1,128,2048]{3,2,1,0:T(8,128)(2,1)S(1)}, u32[]{:S(2)}, u32[]{:S(2)}) collective-permute-start(bf16[1,1,128,2048]{3,2,1,0:T(8,128)(2,1)} %slice.22), channel_id=1, source_target_pairs={{12,0},{24,12},{36,24},{60,48},{72,60},{84,72},{108,96},{120,108},... | collective-permute-start | bytes 1572872 | tf_op jit(solution)/shard_map/ppermute | solution.py:38
  28.3 1.3 %copy-start.2 = (bf16[1,1,128,1024]{3,2,1,0:T(8,128)(2,1)}, bf16[1,1,128,1024]{3,2,1,0:T(8,128)(2,1)S(1)}, u32[]{:S(2)}) copy-start(bf16[1,1,128,1024]{3,2,1,0:T(8,128)(2,1)S(1)} %collective-permute-done.9) | copy-start | bytes 786436
  28.3 33.1 %collective-permute-start.3 = (bf16[1,1,128,1024]{3,2,1,0:T(8,128)(2,1)}, bf16[1,1,128,1024]{3,2,1,0:T(8,128)(2,1)}, u32[]{:S(2)}, u32[]{:S(2)}) collective-permute-start(bf16[1,1,128,1024]{3,2,1,0:T(8,128)(2,1)} %get-tuple-element.12), channel_id=1, source_target_pairs={{0,24},{48,72},{96,120},{144,168},{192,216},{240,264},{288,312},{3... | collective-permute-start | bytes 786440 | tf_op jit(solution)/shard_map/ppermute | solution.py:38
  29.6 33.7 %collective-permute-start.8 = (bf16[1,1,128,1024]{3,2,1,0:T(8,128)(2,1)S(1)}, bf16[1,1,128,1024]{3,2,1,0:T(8,128)(2,1)S(1)}, u32[]{:S(2)}, u32[]{:S(2)}) collective-permute-start(bf16[1,1,128,1024]{3,2,1,0:T(8,128)(2,1)S(1)} %collective-permute-done.7), channel_id=1, source_target_pairs={{36,756},{84,36},{132,84},{180,132},{228,180},{276,228},{324,276},... | collective-permute-start | bytes 786440 | tf_op jit(solution)/shard_map/ppermute | solution.py:38
  59.9 51.6 %collective-permute-start.10 = (bf16[1,1,128,1024]{3,2,1,0:T(8,128)(2,1)}, bf16[1,1,128,1024]{3,2,1,0:T(8,128)(2,1)S(1)}, u32[]{:S(2)}, u32[]{:S(2)}) collective-permute-start(bf16[1,1,128,1024]{3,2,1,0:T(8,128)(2,1)} %copy-done.2), channel_id=1, source_target_pairs={{12,756},{60,36},{108,84},{156,132},{204,180},{252,228},{300,276},... | collective-permute-start | bytes 786440 | tf_op jit(solution)/shard_map/ppermute | solution.py:38
  60.7 0.7 copy-start.3
  61.4 53.4 %collective-permute-start = (bf16[1,1,128,1024]{3,2,1,0:T(8,128)(2,1)S(1)}, bf16[1,1,128,1024]{3,2,1,0:T(8,128)(2,1)S(1)}, u32[]{:S(2)}, u32[]{:S(2)}) collective-permute-start(bf16[1,1,128,1024]{3,2,1,0:T(8,128)(2,1)S(1)} %slice.21), channel_id=1, source_target_pairs={{0,384},{12,396},{24,408},{36,420},{48,432},{60,444},{72,456},{84,... | collective-permute-start | bytes 786440 | tf_op jit(solution)/shard_map/ppermute | solution.py:38
  63.3 51.5 %collective-permute-start.4 = (bf16[1,1,128,1024]{3,2,1,0:T(8,128)(2,1)}, bf16[1,1,128,1024]{3,2,1,0:T(8,128)(2,1)S(1)}, u32[]{:S(2)}, u32[]{:S(2)}) collective-permute-start(bf16[1,1,128,1024]{3,2,1,0:T(8,128)(2,1)} %collective-permute-done.3), channel_id=1, source_target_pairs={{24,756},{72,36},{120,84},{168,132},{216,180},{264,228},{312,276},... | collective-permute-start | bytes 786440 | tf_op jit(solution)/shard_map/ppermute | solution.py:38

commit v2 on v1

--- a/solution.py
+++ b/solution.py
@@ -51,19 +51,16 @@
 
 
 def facts_of(facts_ref):
-    number = lambda value: value.astype(jnp.int32)
-    own = number(facts_ref[0, 3])
-    domain = facts_ref[own, 1]
-    total = jnp.float32(0)
-    count = jnp.float32(0)
-    for b in range(REPLICAS):
-        n = facts_ref[b, 0]
-        total += n
-        count += jnp.where(facts_ref[b, 1] == domain, n, jnp.float32(0))
-    weight = jnp.full((1, HEAD), facts_ref[0, 4 + number(domain)], jnp.float32)
-    total = jnp.full((1, HEAD), total, jnp.float32)
-    count = jnp.full((1, HEAD), count, jnp.float32)
-    return number(facts_ref[own, 0]), number(facts_ref[0, 2]) == NX - 1, weight * total / (DOMAINS * count)
+    facts = facts_ref[...]
+    row = lax.broadcasted_iota(jnp.int32, (REPLICAS, 1), 0).astype(jnp.float32)
+    own = jnp.sum(jnp.where(row == facts[:, 3:4], facts, 0.0), axis=0, keepdims=True)
+    lengths, domains = facts[:, 0:1], facts[:, 1:2]
+    domain = own[:, 1:2]
+    total = jnp.sum(lengths, axis=0, keepdims=True)
+    count = jnp.sum(jnp.where(domains == domain, lengths, 0.0), axis=0, keepdims=True)
+    ids = lax.broadcasted_iota(jnp.int32, (1, DOMAINS), 1).astype(jnp.float32)
+    weight = jnp.sum(jnp.where(ids == domain, own[:, 4 : 4 + DOMAINS], 0.0), axis=1, keepdims=True)
+    return own[:, 0:1].astype(jnp.int32), own[:, 2:3] == NX - 1, weight * total / (DOMAINS * count)
 
 
 def one_group(live_tokens, factor, query, key, value, grad):
@@ -92,9 +89,9 @@
 
 
 def kernel(groups, parts, *refs):
-    facts_ref, q_ref, kv_ref = refs[:3]
+    facts_ref, kv_ref, q_ref = refs[:3]
+    out_q, out_kv, dq, dkv, sem = refs[-5:]
     grads = refs[3:-5]
-    out_q, out_kv, dq, dkv, sem = refs[-5:]
     live_tokens, far, factor = facts_of(facts_ref)
     copies = []
     for at, group in enumerate(groups):
@@ -132,7 +129,6 @@
 
 def attend(groups, parts, facts, arrays, outputs=()):
     vmem = pl.BlockSpec(memory_space=pltpu.VMEM)
-    smem = pl.BlockSpec(memory_space=pltpu.SMEM)
     hbm = pl.BlockSpec(memory_space=pl.ANY)
     count = len(groups)
     operands = (facts, *arrays, *outputs)
@@ -144,7 +140,7 @@
             jax.ShapeDtypeStruct((TOKENS, KV_HEADS * GROUP * HEAD), jnp.bfloat16),
             jax.ShapeDtypeStruct((TOKENS, 2 * KV_HEADS * HEAD), jnp.bfloat16),
         ),
-        in_specs=[smem] + [vmem] * len(arrays) + [hbm] * len(outputs),
+        in_specs=[vmem] * first + [hbm] * len(outputs),
         out_specs=(hbm, hbm),
         scratch_shapes=[
             pltpu.VMEM((count, TOKENS, GROUP * HEAD), jnp.bfloat16),
@@ -187,9 +183,9 @@
     parts += [(1, 3, column(h), column(h)) for h in range(8)]
     parts += [(2, 4, column(h), column(h)) for h in range(8)]
     last = [(0, 1, column(h) + span, column(h)) for h in range(8)]
-    arrays = (q_most, kv, a_all, b_near, cd_near, b_far, c_far)
+    arrays = (kv, q_most, a_all, b_near, cd_near, b_far, c_far)
     outs = attend((0, 1, 2), parts, facts, [flat(a) for a in arrays])
-    arrays = (q_last, kv, cd_near, d_far)
+    arrays = (kv, q_last, cd_near, d_far)
     out_q, out_kv = attend((3,), last, facts, [flat(a) for a in arrays], outs)
     return out_q[None, None], out_kv[None, None]
 

time: 117 us -> 117 us (level)
  no operation moved by 1% of the time
where the time goes in v2:
time: 117 us; the launch traced here: 116 us
  starting transfers between devices  49.5 us (42%)
  waiting for transfers between devices  28.3 us (24%)
  blocking collectives  26.8 us (23%)
  Pallas kernels  4.65 us (4%)
  local copies, waits for them, and re-layouts  4.6 us (4%)
  between operations  2.16 us (2%)
    ppermute x11, starting transfers between devices, moved(): return lax.ppermute(array, 'section', section_pairs(move))  49.5 us
    ppermute x11, waiting for transfers between devices, moved(): return lax.ppermute(array, 'section', section_pairs(move))  28.3 us
    all_to_all x1, blocking collectives, body(): facts = lax.all_to_all(facts, 'dp', 0, 0, tiled=True)  26.8 us
    pallas_call x2, Pallas kernels, attend(): pl.pallas_call(functools.partial(kernel, groups, parts), out_shape=(jax.S...  4.65 us
    slice x2, local copies, waits for them, and re-layouts, body(): upstream[..., first * span:(first + count) * span]  2.89 us
  transfers between devices with their start and end apart: 11, of which 1 were waited for; matrix products, arithmetic and copies ran while one was open for 2% of the time, Pallas kernels for 3%

profile of v2, /device:TPU:36, one launch (start us, length us, event | category | flops | bytes accessed | tf_op | source)
XLA Modules:
  0.0 116.1 jit_solution(16369593762072929980)
XLA Ops:
  0.6 2.1 %fusion = (bf16[1,1,128,1024]{3,2,1,0:T(8,128)(2,1)S(1)}, bf16[1,1,128,1024]{3,2,1,0:T(8,128)(2,1)S(1)}, bf16[1,1,128,1024]{3,2,1,0:T(8,128)(2,1)}, bf16[1,1,128,1024]{3,2,1,0:T(8,128)(2,1)S(1)}) fusion(bf16[1,1,128,4096]{3,2,1,0:T(8,128)(2,1)} %param.8), kind=kLoop, calls=%fused_computation.3 | loop fusion | bytes 2097152 | tf_op jit(solution)/shard_map/slice | solution.py:166
  2.7 2.6 %collective-permute-start.7 = (bf16[1,1,128,1024]{3,2,1,0:T(8,128)(2,1)S(1)}, bf16[1,1,128,1024]{3,2,1,0:T(8,128)(2,1)S(1)}, u32[]{:S(2)}, u32[]{:S(2)}) collective-permute-start(bf16[1,1,128,1024]{3,2,1,0:T(8,128)(2,1)S(1)} %get-tuple-element.13), channel_id=1, source_target_pairs={{0,36},{12,0},{24,12},{36,24},{48,84},{60,48},{72,60},{84,72},{96,... | collective-permute-start | bytes 786440 | tf_op jit(solution)/shard_map/ppermute | solution.py:38
  5.3 0.9 slice.24
  6.2 2.0 %collective-permute-start.5 = (bf16[1,1,128,3072]{3,2,1,0:T(8,128)(2,1)}, bf16[1,1,128,3072]{3,2,1,0:T(8,128)(2,1)S(1)}, u32[]{:S(2)}, u32[]{:S(2)}) collective-permute-start(bf16[1,1,128,3072]{3,2,1,0:T(8,128)(2,1)} %slice.24), channel_id=1, source_target_pairs={{0,384},{12,396},{24,408},{36,420},{48,432},{60,444},{72,456},{84,... | collective-permute-start | bytes 2359304 | tf_op jit(solution)/shard_map/ppermute | solution.py:38
  8.2 0.7 collective-permute-start.9
  8.9 12.0 %collective-permute-start.6 = (bf16[1,1,128,1024]{3,2,1,0:T(8,128)(2,1)S(1)}, bf16[1,1,128,1024]{3,2,1,0:T(8,128)(2,1)S(1)}, u32[]{:S(2)}, u32[]{:S(2)}) collective-permute-start(bf16[1,1,128,1024]{3,2,1,0:T(8,128)(2,1)S(1)} %get-tuple-element.11), channel_id=1, source_target_pairs={{0,756},{12,0},{24,12},{36,24},{48,36},{60,48},{72,60},{84,72},{96... | collective-permute-start | bytes 786440 | tf_op jit(solution)/shard_map/ppermute | solution.py:38
  21.0 1.9 %collective-permute-start = (bf16[1,1,128,1024]{3,2,1,0:T(8,128)(2,1)}, bf16[1,1,128,1024]{3,2,1,0:T(8,128)(2,1)S(1)}, u32[]{:S(2)}, u32[]{:S(2)}) collective-permute-start(bf16[1,1,128,1024]{3,2,1,0:T(8,128)(2,1)} %param.7), channel_id=1, source_target_pairs={{0,384},{12,396},{24,408},{36,420},{48,432},{60,444},{72,456},{84,... | collective-permute-start | bytes 786440 | tf_op jit(solution)/shard_map/ppermute | solution.py:38
  22.9 0.8 slice.22
  23.7 0.0 collective-permute-done.7
  23.7 4.6 %collective-permute-start.2 = (bf16[1,1,128,2048]{3,2,1,0:T(8,128)(2,1)}, bf16[1,1,128,2048]{3,2,1,0:T(8,128)(2,1)S(1)}, u32[]{:S(2)}, u32[]{:S(2)}) collective-permute-start(bf16[1,1,128,2048]{3,2,1,0:T(8,128)(2,1)} %slice.22), channel_id=1, source_target_pairs={{12,0},{24,12},{36,24},{60,48},{72,60},{84,72},{108,96},{120,108},... | collective-permute-start | bytes 1572872 | tf_op jit(solution)/shard_map/ppermute | solution.py:38
  28.3 0.0 collective-permute-done.9
  28.3 1.3 %collective-permute-start.3 = (bf16[1,1,128,1024]{3,2,1,0:T(8,128)(2,1)}, bf16[1,1,128,1024]{3,2,1,0:T(8,128)(2,1)}, u32[]{:S(2)}, u32[]{:S(2)}) collective-permute-start(bf16[1,1,128,1024]{3,2,1,0:T(8,128)(2,1)} %get-tuple-element.12), channel_id=1, source_target_pairs={{0,24},{48,72},{96,120},{144,168},{192,216},{240,264},{288,312},{3... | collective-permute-start | bytes 786440 | tf_op jit(solution)/shard_map/ppermute | solution.py:38
  29.6 0.0 collective-permute-done.6
  29.6 0.7 collective-permute-start.8
  31.6 28.2 %collective-permute-done = bf16[1,1,128,1024]{3,2,1,0:T(8,128)(2,1)S(1)} collective-permute-done((bf16[1,1,128,1024]{3,2,1,0:T(8,128)(2,1)}, bf16[1,1,128,1024]{3,2,1,0:T(8,128)(2,1)S(1)}, u32[]{:S(2)}, u32[]{:S(2)}) %collective-permute-start) | collective-permute-done | bytes 262176 | tf_op jit(solution)/shard_map/ppermute | solution.py:38
  59.9 0.7 collective-permute-start.10
  60.5 0.1 add_convert_fusion
  60.7 0.0 copy-start.3
  60.7 0.6 copy-done.3
  61.3 0.1 pad.2.clone
  61.4 0.0 collective-permute-done.3
  61.4 1.9 %collective-permute-start.1 = (bf16[1,1,128,1024]{3,2,1,0:T(8,128)(2,1)S(1)}, bf16[1,1,128,1024]{3,2,1,0:T(8,128)(2,1)S(1)}, u32[]{:S(2)}, u32[]{:S(2)}) collective-permute-start(bf16[1,1,128,1024]{3,2,1,0:T(8,128)(2,1)S(1)} %slice.21), channel_id=1, source_target_pairs={{0,384},{12,396},{24,408},{36,420},{48,432},{60,444},{72,456},{84,... | collective-permute-start | bytes 786440 | tf_op jit(solution)/shard_map/ppermute | solution.py:38
  63.3 0.0 collective-permute-done.8
  63.3 21.2 %collective-permute-start.4 = (bf16[1,1,128,1024]{3,2,1,0:T(8,128)(2,1)}, bf16[1,1,128,1024]{3,2,1,0:T(8,128)(2,1)S(1)}, u32[]{:S(2)}, u32[]{:S(2)}) collective-permute-start(bf16[1,1,128,1024]{3,2,1,0:T(8,128)(2,1)} %collective-permute-done.3), channel_id=1, source_target_pairs={{24,756},{72,36},{120,84},{168,132},{216,180},{264,228},{312,276},... | collective-permute-start | bytes 786440 | tf_op jit(solution)/shard_map/ppermute | solution.py:38
  84.5 0.1 maximum_bitcast_fusion
  84.6 26.8 %all_to_all.11 = f32[12,1,11]{2,1,0:T(1,128)S(1)} all-to-all(f32[12,1,11]{2,1,0:T(1,128)S(1)} %copy.10), channel_id=1, replica_groups=mesh['section'=64,'dp'=12] {'dp'}, dimensions={0} | all-to-all | bytes 1056 | tf_op jit(solution)/shard_map/all_to_all | solution.py:179
  111.4 0.0 collective-permute-done.10
  111.4 0.0 collective-permute-done.2
  111.4 0.0 collective-permute-done.5
  111.5 3.0 %shard_map.77 = (bf16[128,4096]{1,0:T(8,128)(2,1)}, bf16[128,1024]{1,0:T(8,128)(2,1)}) custom-call(f32[12,11]{1,0:T(8,128)S(1)} %bitcast.28, bf16[128,1024]{1,0:T(8,128)(2,1)S(1)} %bitcast.19, bf16[128,3072]{1,0:T(8,128)(2,1)S(1)} %bitcast.21, bf16[128,1024]{1,0:T(8,128)(2,1)S(1)} %bitcast.23, bf16[128,1024]{1,0:T(8,128)(2,1)S(1)} %bitcast.22, ...), custom_call_target="tpu_custom_call" | custom-call | flops 503316480 | bytes 2359296 | tf_op jit(solution)/shard_map/pallas_call | solution.py:137
  114.4 0.0 collective-permute-done.1
  114.5 1.7 %shard_map.78 = (bf16[128,4096]{1,0:T(8,128)(2,1)}, bf16[128,1024]{1,0:T(8,128)(2,1)}) custom-call(f32[12,11]{1,0:T(8,128)S(1)} %bitcast.29, bf16[128,1024]{1,0:T(8,128)(2,1)S(1)} %bitcast.20, bf16[128,1024]{1,0:T(8,128)(2,1)S(1)} %bitcast.26, bf16[128,2048]{1,0:T(8,128)(2,1)S(1)} %bitcast.18, ...), custom_call_target="tpu_custom_call", output_to_operand_aliasing={{0}: (5, {}), {1}: (6, {})} | custom-call | flops 167772160 | bytes 786432 | tf_op jit(solution)/shard_map/pallas_call | solution.py:137
  (12 shorter events, 0.1 us)
Async XLA Ops:
  0.6 4.6 %copy-start.1 = (bf16[1,1,128,4096]{3,2,1,0:T(8,128)(2,1)S(1)}, bf16[1,1,128,4096]{3,2,1,0:T(8,128)(2,1)}, u32[]{:S(2)}) copy-start(bf16[1,1,128,4096]{3,2,1,0:T(8,128)(2,1)} %param.6) | copy-start | bytes 3145732
  2.7 20.2 %copy-start = (bf16[1,1,128,4096]{3,2,1,0:T(8,128)(2,1)S(1)}, bf16[1,1,128,4096]{3,2,1,0:T(8,128)(2,1)}, u32[]{:S(2)}) copy-start(bf16[1,1,128,4096]{3,2,1,0:T(8,128)(2,1)} %param.8) | copy-start | bytes 3145732
  2.7 21.1 %collective-permute-start.7 = (bf16[1,1,128,1024]{3,2,1,0:T(8,128)(2,1)S(1)}, bf16[1,1,128,1024]{3,2,1,0:T(8,128)(2,1)S(1)}, u32[]{:S(2)}, u32[]{:S(2)}) collective-permute-start(bf16[1,1,128,1024]{3,2,1,0:T(8,128)(2,1)S(1)} %get-tuple-element.13), channel_id=1, source_target_pairs={{0,36},{12,0},{24,12},{36,24},{48,84},{60,48},{72,60},{84,72},{96,... | collective-permute-start | bytes 786440 | tf_op jit(solution)/shard_map/ppermute | solution.py:38
  6.2 105.2 %collective-permute-start.5 = (bf16[1,1,128,3072]{3,2,1,0:T(8,128)(2,1)}, bf16[1,1,128,3072]{3,2,1,0:T(8,128)(2,1)S(1)}, u32[]{:S(2)}, u32[]{:S(2)}) collective-permute-start(bf16[1,1,128,3072]{3,2,1,0:T(8,128)(2,1)} %slice.24), channel_id=1, source_target_pairs={{0,384},{12,396},{24,408},{36,420},{48,432},{60,444},{72,456},{84,... | collective-permute-start | bytes 2359304 | tf_op jit(solution)/shard_map/ppermute | solution.py:38
  8.2 20.1 %collective-permute-start.9 = (bf16[1,1,128,1024]{3,2,1,0:T(8,128)(2,1)S(1)}, bf16[1,1,128,1024]{3,2,1,0:T(8,128)(2,1)S(1)}, u32[]{:S(2)}, u32[]{:S(2)}) collective-permute-start(bf16[1,1,128,1024]{3,2,1,0:T(8,128)(2,1)S(1)} %get-tuple-element.10), channel_id=1, source_target_pairs={{0,12},{48,60},{96,108},{144,156},{192,204},{240,252},{288,300},{3... | collective-permute-start | bytes 786440 | tf_op jit(solution)/shard_map/ppermute | solution.py:38
  8.9 20.7 %collective-permute-start.6 = (bf16[1,1,128,1024]{3,2,1,0:T(8,128)(2,1)S(1)}, bf16[1,1,128,1024]{3,2,1,0:T(8,128)(2,1)S(1)}, u32[]{:S(2)}, u32[]{:S(2)}) collective-permute-start(bf16[1,1,128,1024]{3,2,1,0:T(8,128)(2,1)S(1)} %get-tuple-element.11), channel_id=1, source_target_pairs={{0,756},{12,0},{24,12},{36,24},{48,36},{60,48},{72,60},{84,72},{96... | collective-permute-start | bytes 786440 | tf_op jit(solution)/shard_map/ppermute | solution.py:38
  21.0 38.9 %collective-permute-start = (bf16[1,1,128,1024]{3,2,1,0:T(8,128)(2,1)}, bf16[1,1,128,1024]{3,2,1,0:T(8,128)(2,1)S(1)}, u32[]{:S(2)}, u32[]{:S(2)}) collective-permute-start(bf16[1,1,128,1024]{3,2,1,0:T(8,128)(2,1)} %param.7), channel_id=1, source_target_pairs={{0,384},{12,396},{24,408},{36,420},{48,432},{60,444},{72,456},{84,... | collective-permute-start | bytes 786440 | tf_op jit(solution)/shard_map/ppermute | solution.py:38
  23.7 87.7 %collective-permute-start.2 = (bf16[1,1,128,2048]{3,2,1,0:T(8,128)(2,1)}, bf16[1,1,128,2048]{3,2,1,0:T(8,128)(2,1)S(1)}, u32[]{:S(2)}, u32[]{:S(2)}) collective-permute-start(bf16[1,1,128,2048]{3,2,1,0:T(8,128)(2,1)} %slice.22), channel_id=1, source_target_pairs={{12,0},{24,12},{36,24},{60,48},{72,60},{84,72},{108,96},{120,108},... | collective-permute-start | bytes 1572872 | tf_op jit(solution)/shard_map/ppermute | solution.py:38
  28.3 1.3 %copy-start.2 = (bf16[1,1,128,1024]{3,2,1,0:T(8,128)(2,1)}, bf16[1,1,128,1024]{3,2,1,0:T(8,128)(2,1)S(1)}, u32[]{:S(2)}) copy-start(bf16[1,1,128,1024]{3,2,1,0:T(8,128)(2,1)S(1)} %collective-permute-done.9) | copy-start | bytes 786436
  28.3 33.1 %collective-permute-start.3 = (bf16[1,1,128,1024]{3,2,1,0:T(8,128)(2,1)}, bf16[1,1,128,1024]{3,2,1,0:T(8,128)(2,1)}, u32[]{:S(2)}, u32[]{:S(2)}) collective-permute-start(bf16[1,1,128,1024]{3,2,1,0:T(8,128)(2,1)} %get-tuple-element.12), channel_id=1, source_target_pairs={{0,24},{48,72},{96,120},{144,168},{192,216},{240,264},{288,312},{3... | collective-permute-start | bytes 786440 | tf_op jit(solution)/shard_map/ppermute | solution.py:38
  29.6 33.7 %collective-permute-start.8 = (bf16[1,1,128,1024]{3,2,1,0:T(8,128)(2,1)S(1)}, bf16[1,1,128,1024]{3,2,1,0:T(8,128)(2,1)S(1)}, u32[]{:S(2)}, u32[]{:S(2)}) collective-permute-start(bf16[1,1,128,1024]{3,2,1,0:T(8,128)(2,1)S(1)} %collective-permute-done.7), channel_id=1, source_target_pairs={{36,756},{84,36},{132,84},{180,132},{228,180},{276,228},{324,276},... | collective-permute-start | bytes 786440 | tf_op jit(solution)/shard_map/ppermute | solution.py:38
  59.9 51.6 %collective-permute-start.10 = (bf16[1,1,128,1024]{3,2,1,0:T(8,128)(2,1)}, bf16[1,1,128,1024]{3,2,1,0:T(8,128)(2,1)S(1)}, u32[]{:S(2)}, u32[]{:S(2)}) collective-permute-start(bf16[1,1,128,1024]{3,2,1,0:T(8,128)(2,1)} %copy-done.2), channel_id=1, source_target_pairs={{12,756},{60,36},{108,84},{156,132},{204,180},{252,228},{300,276},... | collective-permute-start | bytes 786440 | tf_op jit(solution)/shard_map/ppermute | solution.py:38
  60.7 0.7 copy-start.3
  61.4 53.1 %collective-permute-start.1 = (bf16[1,1,128,1024]{3,2,1,0:T(8,128)(2,1)S(1)}, bf16[1,1,128,1024]{3,2,1,0:T(8,128)(2,1)S(1)}, u32[]{:S(2)}, u32[]{:S(2)}) collective-permute-start(bf16[1,1,128,1024]{3,2,1,0:T(8,128)(2,1)S(1)} %slice.21), channel_id=1, source_target_pairs={{0,384},{12,396},{24,408},{36,420},{48,432},{60,444},{72,456},{84,... | collective-permute-start | bytes 786440 | tf_op jit(solution)/shard_map/ppermute | solution.py:38
  63.3 51.1 %collective-permute-start.4 = (bf16[1,1,128,1024]{3,2,1,0:T(8,128)(2,1)}, bf16[1,1,128,1024]{3,2,1,0:T(8,128)(2,1)S(1)}, u32[]{:S(2)}, u32[]{:S(2)}) collective-permute-start(bf16[1,1,128,1024]{3,2,1,0:T(8,128)(2,1)} %collective-permute-done.3), channel_id=1, source_target_pairs={{24,756},{72,36},{120,84},{168,132},{216,180},{264,228},{312,276},... | collective-permute-start | bytes 786440 | tf_op jit(solution)/shard_map/ppermute | solution.py:38

commit v3 on v2

--- a/solution.py
+++ b/solution.py
@@ -34,33 +34,47 @@
     return pairs
 
 
+def device_pairs(move):
+    pairs = []
+    for y in range(NY):
+        for z in range(NZ):
+            for x in range(NX):
+                for r in range(REPLICAS):
+                    to = move(y, z, r)
+                    if to is not None:
+                        ty, tr = to
+                        section = lambda v: ((v % NY) * NZ + z) * NX + x
+                        pairs.append((section(y) * REPLICAS + r, section(ty) * REPLICAS + tr))
+    return pairs
+
+
+def moved_each(array, move):
+    return lax.ppermute(array, ("section", "dp"), device_pairs(move))
+
+
+def turned(y, z, replica):
+    return (z == 1) & (replica % 2 == 0) & (y % 4 == 1)
+
+
 def moved(array, move):
     return lax.ppermute(array, "section", section_pairs(move))
 
 
 def opposite(y, z, x):
     return y + 4, z, x
-
-
-def previous(y, z, x):
-    return (y, z, x - 1) if x else (y - 1 + z, z + 1, 3)
-
-
-def x_ring(y, z, x):
-    return y, z, x - 1
 
 
 def facts_of(facts_ref):
     facts = facts_ref[...]
     row = lax.broadcasted_iota(jnp.int32, (REPLICAS, 1), 0).astype(jnp.float32)
-    own = jnp.sum(jnp.where(row == facts[:, 3:4], facts, 0.0), axis=0, keepdims=True)
+    own = jnp.sum(jnp.where(row == facts[:, 4:5], facts, 0.0), axis=0, keepdims=True)
     lengths, domains = facts[:, 0:1], facts[:, 1:2]
     domain = own[:, 1:2]
     total = jnp.sum(lengths, axis=0, keepdims=True)
     count = jnp.sum(jnp.where(domains == domain, lengths, 0.0), axis=0, keepdims=True)
     ids = lax.broadcasted_iota(jnp.int32, (1, DOMAINS), 1).astype(jnp.float32)
-    weight = jnp.sum(jnp.where(ids == domain, own[:, 4 : 4 + DOMAINS], 0.0), axis=1, keepdims=True)
-    return own[:, 0:1].astype(jnp.int32), own[:, 2:3] == NX - 1, weight * total / (DOMAINS * count)
+    weight = jnp.sum(jnp.where(ids == domain, own[:, 5 : 5 + DOMAINS], 0.0), axis=1, keepdims=True)
+    return own[:, 0:1].astype(jnp.int32), own[:, 2:3] > 0.5, own[:, 3:4] > 0.5, weight * total / (DOMAINS * count)
 
 
 def one_group(live_tokens, factor, query, key, value, grad):
@@ -88,16 +102,21 @@
     )
 
 
-def kernel(groups, parts, *refs):
+def kernel(groups, parts, two_ways, *refs):
     facts_ref, kv_ref, q_ref = refs[:3]
     out_q, out_kv, dq, dkv, sem = refs[-5:]
-    grads = refs[3:-5]
-    live_tokens, far, factor = facts_of(facts_ref)
+    n_grads = 1 + max(max(p[0], -1 if p[1] is None else p[1]) for p in parts)
+    grads = refs[3 : 3 + n_grads]
+    turned_ref = refs[3 + n_grads] if two_ways else None
+    live_tokens, far, turn, factor = facts_of(facts_ref)
     copies = []
     for at, group in enumerate(groups):
         queries, gradients = [], []
         for head in range(at * GROUP, (at + 1) * GROUP):
-            queries.append(q_ref[:, head * HEAD : (head + 1) * HEAD])
+            q = q_ref[:, head * HEAD : (head + 1) * HEAD]
+            if two_ways:
+                q = jnp.where(turn, turned_ref[:, head * HEAD : (head + 1) * HEAD], q)
+            queries.append(q)
             plain, other, column, other_column = parts[head]
             g = grads[plain][:, column : column + HEAD]
             if other is not None:
@@ -127,7 +146,7 @@
         copy.wait()
 
 
-def attend(groups, parts, facts, arrays, outputs=()):
+def attend(groups, parts, facts, arrays, outputs=(), two_ways=False):
     vmem = pl.BlockSpec(memory_space=pltpu.VMEM)
     hbm = pl.BlockSpec(memory_space=pl.ANY)
     count = len(groups)
@@ -135,7 +154,7 @@
     first = 1 + len(arrays)
     elements = count * GROUP * TOKENS * HEAD
     return pl.pallas_call(
-        functools.partial(kernel, groups, parts),
+        functools.partial(kernel, groups, parts, two_ways),
         out_shape=(
             jax.ShapeDtypeStruct((TOKENS, KV_HEADS * GROUP * HEAD), jnp.bfloat16),
             jax.ShapeDtypeStruct((TOKENS, 2 * KV_HEADS * HEAD), jnp.bfloat16),
@@ -158,35 +177,40 @@
 
 
 def body(stash_q, stash_kv, upstream, lengths, domains, domain_weight):
-    x = lax.axis_index("section") % NX
+    section = lax.axis_index("section")
+    x = section % NX
     span = GROUP * HEAD
     kv = moved(stash_kv, opposite)
     q_most = moved(stash_q[..., : 3 * span], opposite)
-    q_last = moved(stash_q[..., 3 * span :], opposite)
-    part = lambda first, count: upstream[..., first * span : (first + count) * span]
-    b_near = moved(part(1, 1), x_ring)
-    c_mid = moved(part(2, 1), lambda y, z, x: (y, z, 1) if x == 0 else None)
-    d_mid = moved(part(3, 1), lambda y, z, x: (y, z, 2) if x == 0 else None)
-    cd_near = moved(part(2, 2), lambda y, z, x: (y, z, x - 1) if x else None)
-    a_all = moved(part(0, 1), previous)
-    b_far = moved(b_near, across(3))
+    last_part = stash_q[..., 3 * span :]
+    q_last = moved_each(last_part, lambda y, z, r: None if turned(y, z, r) else (y + 4, r))
+    q_mid = moved_each(last_part, lambda y, z, r: (y + 1, r ^ 2) if turned(y, z, r) else None)
+    q_turned = moved_each(q_mid, lambda y, z, r: (y + 3, r ^ 2) if turned(y - 1, z, r) else None)
+    part = lambda group: upstream[..., group * span : (group + 1) * span]
+    beside = lambda column: lambda y, z, x: (y, z, column) if x == 0 else None
+    b_mid = moved(part(1), beside(3))
+    c_mid = moved(part(2), beside(1))
+    d_mid = moved(part(3), beside(2))
+    near = moved(upstream, lambda y, z, x: (y, z, x - 1) if x else None)
+    a_far = moved(part(0), across(0))
+    b_far = moved(b_mid, across(3))
     c_far = moved(c_mid, across(1))
     d_far = moved(d_mid, across(2))
-    own = jnp.concatenate([lengths, domains, x[None]]).astype(jnp.float32)
+    y, z, replica = section // (NZ * NX), section // NX % NZ, lax.axis_index("dp")
+    flags = jnp.stack([x == NX - 1, turned(y, z, replica)])
+    own = jnp.concatenate([lengths, domains, flags]).astype(jnp.float32)
     to = jnp.arange(REPLICAS, dtype=jnp.float32)[:, None]
     row = lambda v: jnp.broadcast_to(v[None], (REPLICAS, v.shape[0]))
     facts = jnp.concatenate([row(own), to, row(domain_weight)], axis=1)
     facts = lax.all_to_all(facts, "dp", 0, 0, tiled=True)
     flat = lambda a: a.reshape(a.shape[2:])
     column = lambda h: (h % GROUP) * HEAD
-    parts = [(0, None, column(h), 0) for h in range(8)]
-    parts += [(1, 3, column(h), column(h)) for h in range(8)]
-    parts += [(2, 4, column(h), column(h)) for h in range(8)]
-    last = [(0, 1, column(h) + span, column(h)) for h in range(8)]
-    arrays = (kv, q_most, a_all, b_near, cd_near, b_far, c_far)
+    parts = [(0, 1 + g, column(h) + g * span, column(h)) for g in range(3) for h in range(GROUP)]
+    arrays = (kv, q_most, near, a_far, b_far, c_far)
     outs = attend((0, 1, 2), parts, facts, [flat(a) for a in arrays])
-    arrays = (kv, q_last, cd_near, d_far)
-    out_q, out_kv = attend((3,), last, facts, [flat(a) for a in arrays], outs)
+    last = [(0, 1, column(h) + 3 * span, column(h)) for h in range(GROUP)]
+    arrays = (kv, q_last, near, d_far, q_turned)
+    out_q, out_kv = attend((3,), last, facts, [flat(a) for a in arrays], outs, True)
     return out_q[None, None], out_kv[None, None]
 
 

time: 117 us -> 134 us (1.15)
  the two profiles are of different devices: /device:TPU:36 before, /device:TPU:28 now
where the time goes in v3:
time: 134 us
  starting transfers between devices  65.6 us (49%)
  waiting for transfers between devices  36.4 us (27%)
  blocking collectives  21.7 us (16%)
  Pallas kernels  4.77 us (4%)
  local copies, waits for them, and re-layouts  2.98 us (2%)
  between operations  2.21 us (2%)
    ppermute x10, starting transfers between devices, moved(): return lax.ppermute(array, 'section', section_pairs(move))  56.4 us
    ppermute x10, waiting for transfers between devices, moved(): return lax.ppermute(array, 'section', section_pairs(move))  36.4 us
    all_to_all x1, blocking collectives, body(): facts = lax.all_to_all(facts, 'dp', 0, 0, tiled=True)  21.7 us
    ppermute x3, starting transfers between devices, moved_each(): return lax.ppermute(array, ('section', 'dp'), device_pairs(move))  9.15 us
    pallas_call x2, Pallas kernels, attend(): pl.pallas_call(functools.partial(kernel, groups, parts, two_ways), out_sh...  4.77 us
  transfers between devices with their start and end apart: 13, of which 1 were waited for; matrix products, arithmetic and copies ran while one was open for 2% of the time, Pallas kernels for 2%

profile of v3, /device:TPU:28, one launch (start us, length us, event | category | flops | bytes accessed | tf_op | source)
XLA Modules:
  0.0 133.8 jit_solution(13733299510159775837)
XLA Ops:
  0.6 2.6 %collective-permute-start.2 = (bf16[1,1,128,4096]{3,2,1,0:T(8,128)(2,1)}, bf16[1,1,128,4096]{3,2,1,0:T(8,128)(2,1)S(1)}, u32[]{:S(2)}, u32[]{:S(2)}) collective-permute-start(bf16[1,1,128,4096]{3,2,1,0:T(8,128)(2,1)} %param.8), channel_id=1, source_target_pairs={{12,0},{24,12},{36,24},{60,48},{72,60},{84,72},{108,96},{120,108},... | collective-permute-start | bytes 3145736 | tf_op jit(solution)/shard_map/ppermute | solution.py:60
  3.2 1.3 fusion
  4.5 1.4 %collective-permute-start.11 = (bf16[1,1,128,1024]{3,2,1,0:T(8,128)(2,1)S(1)}, bf16[1,1,128,1024]{3,2,1,0:T(8,128)(2,1)}, u32[]{:S(2)}, u32[]{:S(2)}) collective-permute-start(bf16[1,1,128,1024]{3,2,1,0:T(8,128)(2,1)S(1)} %get-tuple-element.10), channel_id=1, source_target_pairs={{0,12},{48,60},{96,108},{144,156},{192,204},{240,252},{288,300},{3... | collective-permute-start | bytes 786440 | tf_op jit(solution)/shard_map/ppermute | solution.py:60
  5.9 1.5 %collective-permute-start.9 = (bf16[1,1,128,1024]{3,2,1,0:T(8,128)(2,1)S(1)}, bf16[1,1,128,1024]{3,2,1,0:T(8,128)(2,1)}, u32[]{:S(2)}, u32[]{:S(2)}) collective-permute-start(bf16[1,1,128,1024]{3,2,1,0:T(8,128)(2,1)S(1)} %get-tuple-element.13), channel_id=1, source_target_pairs={{0,36},{48,84},{96,132},{144,180},{192,228},{240,276},{288,324},{3... | collective-permute-start | bytes 786440 | tf_op jit(solution)/shard_map/ppermute | solution.py:60
  7.3 0.9 slice.20
  8.3 5.0 %collective-permute-start.7 = (bf16[1,1,128,3072]{3,2,1,0:T(8,128)(2,1)}, bf16[1,1,128,3072]{3,2,1,0:T(8,128)(2,1)S(1)}, u32[]{:S(2)}, u32[]{:S(2)}) collective-permute-start(bf16[1,1,128,3072]{3,2,1,0:T(8,128)(2,1)} %slice.20), channel_id=1, source_target_pairs={{0,384},{12,396},{24,408},{36,420},{48,432},{60,444},{72,456},{84,... | collective-permute-start | bytes 2359304 | tf_op jit(solution)/shard_map/ppermute | solution.py:60
  13.3 0.7 collective-permute-start.8
  14.0 0.0 collective-permute-done.11
  14.0 4.7 %collective-permute-start = (bf16[1,1,128,1024]{3,2,1,0:T(8,128)(2,1)S(1)}, bf16[1,1,128,1024]{3,2,1,0:T(8,128)(2,1)S(1)}, u32[]{:S(2)}, u32[]{:S(2)}) collective-permute-start(bf16[1,1,128,1024]{3,2,1,0:T(8,128)(2,1)S(1)} %copy-done.1), channel_id=1, source_target_pairs={{0,384},{12,396},{24,408},{36,420},{48,432},{60,444},{72,456},{84,... | collective-permute-start | bytes 786440 | tf_op jit(solution)/shard_map/ppermute | solution.py:60
  18.7 0.0 collective-permute-done.9
  18.8 1.3 collective-permute-start.3
  20.1 0.0 collective-permute-done.8
  20.1 1.4 %collective-permute-start.5 = (bf16[1,1,128,1024]{3,2,1,0:T(8,128)(2,1)S(1)}, bf16[1,1,128,1024]{3,2,1,0:T(8,128)(2,1)}, u32[]{:S(2)}, u32[]{:S(2)}) collective-permute-start(bf16[1,1,128,1024]{3,2,1,0:T(8,128)(2,1)S(1)} %slice.18), channel_id=1, source_target_pairs={{144,242},{146,240},{148,246},{150,244},{152,250},{154,248},{156,2... | collective-permute-start | bytes 786440 | tf_op jit(solution)/shard_map/ppermute | solution.py:52
  21.5 36.4 %collective-permute-done = bf16[1,1,128,1024]{3,2,1,0:T(8,128)(2,1)S(1)} collective-permute-done((bf16[1,1,128,1024]{3,2,1,0:T(8,128)(2,1)S(1)}, bf16[1,1,128,1024]{3,2,1,0:T(8,128)(2,1)S(1)}, u32[]{:S(2)}, u32[]{:S(2)}) %collective-permute-start) | collective-permute-done | bytes 262176 | tf_op jit(solution)/shard_map/ppermute | solution.py:60
  57.8 0.7 collective-permute-start.12
  58.5 0.0 collective-permute-done.3
  58.5 0.7 collective-permute-start.10
  60.6 0.1 add_convert_fusion
  60.7 0.1 add_convert_fusion.1
  60.8 0.7 copy-done.2
  61.4 0.1 pad.2.clone
  61.5 0.0 collective-permute-done.5
  61.5 7.1 %collective-permute-start.1 = (bf16[1,1,128,1024]{3,2,1,0:T(8,128)(2,1)S(1)}, bf16[1,1,128,1024]{3,2,1,0:T(8,128)(2,1)S(1)}, u32[]{:S(2)}, u32[]{:S(2)}) collective-permute-start(bf16[1,1,128,1024]{3,2,1,0:T(8,128)(2,1)S(1)} %slice.18), channel_id=1, source_target_pairs={{0,384},{1,385},{2,386},{3,387},{4,388},{5,389},{6,390},{7,391},{8... | collective-permute-start | bytes 786440 | tf_op jit(solution)/shard_map/ppermute | solution.py:52
  68.6 0.0 collective-permute-done.12
  68.6 37.9 %collective-permute-start.4 = (bf16[1,1,128,1024]{3,2,1,0:T(8,128)(2,1)S(1)}, bf16[1,1,128,1024]{3,2,1,0:T(8,128)(2,1)S(1)}, u32[]{:S(2)}, u32[]{:S(2)}) collective-permute-start(bf16[1,1,128,1024]{3,2,1,0:T(8,128)(2,1)S(1)} %collective-permute-done.3), channel_id=1, source_target_pairs={{24,756},{72,36},{120,84},{168,132},{216,180},{264,228},{312,276},... | collective-permute-start | bytes 786440 | tf_op jit(solution)/shard_map/ppermute | solution.py:60
  106.5 0.0 collective-permute-done.10
  106.6 0.7 collective-permute-start.6
  107.3 0.1 maximum_maximum_fusion
  107.3 21.7 %all_to_all.11 = f32[12,1,12]{2,1,0:T(1,128)S(1)} all-to-all(f32[12,1,12]{2,1,0:T(1,128)S(1)} %all_to_all.7), channel_id=1, replica_groups=mesh['section'=64,'dp'=12] {'dp'}, dimensions={0} | all-to-all | bytes 1152 | tf_op jit(solution)/shard_map/all_to_all | solution.py:205
  129.0 3.1 %shard_map.77 = (bf16[128,4096]{1,0:T(8,128)(2,1)}, bf16[128,1024]{1,0:T(8,128)(2,1)}) custom-call(f32[12,12]{1,0:T(8,128)S(1)} %bitcast.27, bf16[128,1024]{1,0:T(8,128)(2,1)S(1)} %bitcast.18, bf16[128,3072]{1,0:T(8,128)(2,1)S(1)} %bitcast.20, bf16[128,4096]{1,0:T(8,128)(2,1)S(1)} %bitcast.16, bf16[128,1024]{1,0:T(8,128)(2,1)S(1)} %bitcast.21, ...), custom_call_target="tpu_custom_call" | custom-call | flops 503316480 | bytes 2359296 | tf_op jit(solution)/shard_map/pallas_call | solution.py:156
  132.1 0.0 collective-permute-done.6
  132.1 1.7 %shard_map.78 = (bf16[128,4096]{1,0:T(8,128)(2,1)}, bf16[128,1024]{1,0:T(8,128)(2,1)}) custom-call(f32[12,12]{1,0:T(8,128)S(1)} %bitcast.28, bf16[128,1024]{1,0:T(8,128)(2,1)S(1)} %bitcast.19, bf16[128,1024]{1,0:T(8,128)(2,1)S(1)} %bitcast.24, bf16[128,4096]{1,0:T(8,128)(2,1)S(1)} %bitcast.17, ...), custom_call_target="tpu_custom_call", output_to_operand_aliasing={{0}: (6, {}), {1}: (7, {})} | custom-call | flops 167772160 | bytes 786432 | tf_op jit(solution)/shard_map/pallas_call | solution.py:156
  (14 shorter events, 0.1 us)
Async XLA Ops:
  0.6 6.7 %copy-start = (bf16[1,1,128,4096]{3,2,1,0:T(8,128)(2,1)S(1)}, bf16[1,1,128,4096]{3,2,1,0:T(8,128)(2,1)}, u32[]{:S(2)}) copy-start(bf16[1,1,128,4096]{3,2,1,0:T(8,128)(2,1)} %param.6) | copy-start | bytes 3145732
  0.6 128.4 %collective-permute-start.2 = (bf16[1,1,128,4096]{3,2,1,0:T(8,128)(2,1)}, bf16[1,1,128,4096]{3,2,1,0:T(8,128)(2,1)S(1)}, u32[]{:S(2)}, u32[]{:S(2)}) collective-permute-start(bf16[1,1,128,4096]{3,2,1,0:T(8,128)(2,1)} %param.8), channel_id=1, source_target_pairs={{12,0},{24,12},{36,24},{60,48},{72,60},{84,72},{108,96},{120,108},... | collective-permute-start | bytes 3145736 | tf_op jit(solution)/shard_map/ppermute | solution.py:60
  4.5 9.5 %collective-permute-start.11 = (bf16[1,1,128,1024]{3,2,1,0:T(8,128)(2,1)S(1)}, bf16[1,1,128,1024]{3,2,1,0:T(8,128)(2,1)}, u32[]{:S(2)}, u32[]{:S(2)}) collective-permute-start(bf16[1,1,128,1024]{3,2,1,0:T(8,128)(2,1)S(1)} %get-tuple-element.10), channel_id=1, source_target_pairs={{0,12},{48,60},{96,108},{144,156},{192,204},{240,252},{288,300},{3... | collective-permute-start | bytes 786440 | tf_op jit(solution)/shard_map/ppermute | solution.py:60
  5.9 8.2 %copy-start.1 = (bf16[1,1,128,1024]{3,2,1,0:T(8,128)(2,1)S(1)}, bf16[1,1,128,1024]{3,2,1,0:T(8,128)(2,1)}, u32[]{:S(2)}) copy-start(bf16[1,1,128,1024]{3,2,1,0:T(8,128)(2,1)} %param.7) | copy-start | bytes 786436
  5.9 12.9 %collective-permute-start.9 = (bf16[1,1,128,1024]{3,2,1,0:T(8,128)(2,1)S(1)}, bf16[1,1,128,1024]{3,2,1,0:T(8,128)(2,1)}, u32[]{:S(2)}, u32[]{:S(2)}) collective-permute-start(bf16[1,1,128,1024]{3,2,1,0:T(8,128)(2,1)S(1)} %get-tuple-element.13), channel_id=1, source_target_pairs={{0,36},{48,84},{96,132},{144,180},{192,228},{240,276},{288,324},{3... | collective-permute-start | bytes 786440 | tf_op jit(solution)/shard_map/ppermute | solution.py:60
  8.3 120.7 %collective-permute-start.7 = (bf16[1,1,128,3072]{3,2,1,0:T(8,128)(2,1)}, bf16[1,1,128,3072]{3,2,1,0:T(8,128)(2,1)S(1)}, u32[]{:S(2)}, u32[]{:S(2)}) collective-permute-start(bf16[1,1,128,3072]{3,2,1,0:T(8,128)(2,1)} %slice.20), channel_id=1, source_target_pairs={{0,384},{12,396},{24,408},{36,420},{48,432},{60,444},{72,456},{84,... | collective-permute-start | bytes 2359304 | tf_op jit(solution)/shard_map/ppermute | solution.py:60
  13.3 6.8 %collective-permute-start.8 = (bf16[1,1,128,1024]{3,2,1,0:T(8,128)(2,1)S(1)}, bf16[1,1,128,1024]{3,2,1,0:T(8,128)(2,1)S(1)}, u32[]{:S(2)}, u32[]{:S(2)}) collective-permute-start(bf16[1,1,128,1024]{3,2,1,0:T(8,128)(2,1)S(1)} %get-tuple-element.11), channel_id=1, source_target_pairs={{0,756},{48,36},{96,84},{144,132},{192,180},{240,228},{288,276},{3... | collective-permute-start | bytes 786440 | tf_op jit(solution)/shard_map/ppermute | solution.py:60
  14.0 43.8 %collective-permute-start = (bf16[1,1,128,1024]{3,2,1,0:T(8,128)(2,1)S(1)}, bf16[1,1,128,1024]{3,2,1,0:T(8,128)(2,1)S(1)}, u32[]{:S(2)}, u32[]{:S(2)}) collective-permute-start(bf16[1,1,128,1024]{3,2,1,0:T(8,128)(2,1)S(1)} %copy-done.1), channel_id=1, source_target_pairs={{0,384},{12,396},{24,408},{36,420},{48,432},{60,444},{72,456},{84,... | collective-permute-start | bytes 786440 | tf_op jit(solution)/shard_map/ppermute | solution.py:60
  18.8 39.8 %collective-permute-start.3 = (bf16[1,1,128,1024]{3,2,1,0:T(8,128)(2,1)S(1)}, bf16[1,1,128,1024]{3,2,1,0:T(8,128)(2,1)S(1)}, u32[]{:S(2)}, u32[]{:S(2)}) collective-permute-start(bf16[1,1,128,1024]{3,2,1,0:T(8,128)(2,1)S(1)} %get-tuple-element.12), channel_id=1, source_target_pairs={{0,24},{48,72},{96,120},{144,168},{192,216},{240,264},{288,312},{3... | collective-permute-start | bytes 786440 | tf_op jit(solution)/shard_map/ppermute | solution.py:60
  20.1 41.4 %collective-permute-start.5 = (bf16[1,1,128,1024]{3,2,1,0:T(8,128)(2,1)S(1)}, bf16[1,1,128,1024]{3,2,1,0:T(8,128)(2,1)}, u32[]{:S(2)}, u32[]{:S(2)}) collective-permute-start(bf16[1,1,128,1024]{3,2,1,0:T(8,128)(2,1)S(1)} %slice.18), channel_id=1, source_target_pairs={{144,242},{146,240},{148,246},{150,244},{152,250},{154,248},{156,2... | collective-permute-start | bytes 786440 | tf_op jit(solution)/shard_map/ppermute | solution.py:52
  57.8 10.8 %collective-permute-start.12 = (bf16[1,1,128,1024]{3,2,1,0:T(8,128)(2,1)}, bf16[1,1,128,1024]{3,2,1,0:T(8,128)(2,1)S(1)}, u32[]{:S(2)}, u32[]{:S(2)}) collective-permute-start(bf16[1,1,128,1024]{3,2,1,0:T(8,128)(2,1)} %collective-permute-done.11), channel_id=1, source_target_pairs={{12,756},{60,36},{108,84},{156,132},{204,180},{252,228},{300,276},... | collective-permute-start | bytes 786440 | tf_op jit(solution)/shard_map/ppermute | solution.py:60
  58.5 48.0 %collective-permute-start.10 = (bf16[1,1,128,1024]{3,2,1,0:T(8,128)(2,1)}, bf16[1,1,128,1024]{3,2,1,0:T(8,128)(2,1)S(1)}, u32[]{:S(2)}, u32[]{:S(2)}) collective-permute-start(bf16[1,1,128,1024]{3,2,1,0:T(8,128)(2,1)} %collective-permute-done.9), channel_id=1, source_target_pairs={{36,756},{84,36},{132,84},{180,132},{228,180},{276,228},{324,276},... | collective-permute-start | bytes 786440 | tf_op jit(solution)/shard_map/ppermute | solution.py:60
  60.8 0.7 copy-start.2
  61.5 70.6 %collective-permute-start.1 = (bf16[1,1,128,1024]{3,2,1,0:T(8,128)(2,1)S(1)}, bf16[1,1,128,1024]{3,2,1,0:T(8,128)(2,1)S(1)}, u32[]{:S(2)}, u32[]{:S(2)}) collective-permute-start(bf16[1,1,128,1024]{3,2,1,0:T(8,128)(2,1)S(1)} %slice.18), channel_id=1, source_target_pairs={{0,384},{1,385},{2,386},{3,387},{4,388},{5,389},{6,390},{7,391},{8... | collective-permute-start | bytes 786440 | tf_op jit(solution)/shard_map/ppermute | solution.py:52
  68.6 63.5 %collective-permute-start.4 = (bf16[1,1,128,1024]{3,2,1,0:T(8,128)(2,1)S(1)}, bf16[1,1,128,1024]{3,2,1,0:T(8,128)(2,1)S(1)}, u32[]{:S(2)}, u32[]{:S(2)}) collective-permute-start(bf16[1,1,128,1024]{3,2,1,0:T(8,128)(2,1)S(1)} %collective-permute-done.3), channel_id=1, source_target_pairs={{24,756},{72,36},{120,84},{168,132},{216,180},{264,228},{312,276},... | collective-permute-start | bytes 786440 | tf_op jit(solution)/shard_map/ppermute | solution.py:60
  106.6 25.6 %collective-permute-start.6 = (bf16[1,1,128,1024]{3,2,1,0:T(8,128)(2,1)}, bf16[1,1,128,1024]{3,2,1,0:T(8,128)(2,1)S(1)}, u32[]{:S(2)}, u32[]{:S(2)}) collective-permute-start(bf16[1,1,128,1024]{3,2,1,0:T(8,128)(2,1)} %collective-permute-done.5), channel_id=1, source_target_pairs={{240,530},{242,528},{244,534},{246,532},{248,538},{250,536},{252,5... | collective-permute-start | bytes 786440 | tf_op jit(solution)/shard_map/ppermute | solution.py:52

commit v4 on v3

--- a/solution.py
+++ b/solution.py
@@ -172,6 +172,31 @@
     )(*operands)
 
 
+def cut_kernel(spans, *refs):
+    sources, pieces, sem = refs[:2], refs[2:-1], refs[-1]
+    copies = []
+    for n, (piece, (source, first, last)) in enumerate(zip(pieces, spans)):
+        copies.append(pltpu.make_async_copy(sources[source].at[:, first:last], piece, sem.at[n]))
+        copies[-1].start()
+    for copy in copies:
+        copy.wait()
+
+
+def cut(query, grad):
+    span = GROUP * HEAD
+    spans = [(0, 0, 3 * span), (0, 3 * span, 4 * span)] + [(1, g * span, (g + 1) * span) for g in range(KV_HEADS)]
+    return pl.pallas_call(
+        functools.partial(cut_kernel, spans),
+        out_shape=[jax.ShapeDtypeStruct((TOKENS, last - first), jnp.bfloat16) for _, first, last in spans],
+        in_specs=[pl.BlockSpec(memory_space=pl.ANY)] * 2,
+        out_specs=[pl.BlockSpec(memory_space=pltpu.VMEM)] * len(spans),
+        scratch_shapes=[pltpu.SemaphoreType.DMA((len(spans),))],
+        compiler_params=pltpu.CompilerParams(vmem_limit_bytes=24 << 20),
+        cost_estimate=pl.CostEstimate(flops=0, bytes_accessed=4 * TOKENS * 8 * span, transcendentals=0),
+        name="cut",
+    )(query, grad)
+
+
 def across(column):
     return lambda y, z, x: (y - 1 + z, z + 1, 3) if x == column else None
 
@@ -181,12 +206,12 @@
     x = section % NX
     span = GROUP * HEAD
     kv = moved(stash_kv, opposite)
-    q_most = moved(stash_q[..., : 3 * span], opposite)
-    last_part = stash_q[..., 3 * span :]
+    first_part, last_part, *parts = [a[None, None] for a in cut(stash_q[0, 0], upstream[0, 0])]
+    q_most = moved(first_part, opposite)
     q_last = moved_each(last_part, lambda y, z, r: None if turned(y, z, r) else (y + 4, r))
     q_mid = moved_each(last_part, lambda y, z, r: (y + 1, r ^ 2) if turned(y, z, r) else None)
     q_turned = moved_each(q_mid, lambda y, z, r: (y + 3, r ^ 2) if turned(y - 1, z, r) else None)
-    part = lambda group: upstream[..., group * span : (group + 1) * span]
+    part = lambda group: parts[group]
     beside = lambda column: lambda y, z, x: (y, z, column) if x == 0 else None
     b_mid = moved(part(1), beside(3))
     c_mid = moved(part(2), beside(1))

time: 134 us -> 138 us (1.030)
  the two profiles are of different devices: /device:TPU:28 before, /device:TPU:44 now
where the time goes in v4:
time: 138 us
  starting transfers between devices  63.2 us (46%)
  waiting for transfers between devices  40 us (29%)
  blocking collectives  22.9 us (17%)
  Pallas kernels  5.86 us (4%)
  local copies, waits for them, and re-layouts  3.19 us (2%)
  between operations  2.2 us (2%)
    ppermute x10, starting transfers between devices, moved(): return lax.ppermute(array, 'section', section_pairs(move))  58.3 us
    ppermute x10, waiting for transfers between devices, moved(): return lax.ppermute(array, 'section', section_pairs(move))  40 us
    all_to_all x1, blocking collectives, body(): facts = lax.all_to_all(facts, 'dp', 0, 0, tiled=True)  22.9 us
    ppermute x3, starting transfers between devices, moved_each(): return lax.ppermute(array, ('section', 'dp'), device_pairs(move))  4.94 us
    pallas_call x2, Pallas kernels, attend(): pl.pallas_call(functools.partial(kernel, groups, parts, two_ways), out_sh...  4.78 us
    unnamed x9, local copies, waits for them, and re-layouts  3.1 us
  transfers between devices with their start and end apart: 13, of which 1 were waited for; matrix products, arithmetic and copies ran while one was open for 0% of the time, Pallas kernels for 3%

profile of v4, /device:TPU:44, one launch (start us, length us, event | category | flops | bytes accessed | tf_op | source)
XLA Modules:
  0.0 137.6 jit_solution(11689520316729263763)
XLA Ops:
  0.6 2.4 %collective-permute-start.2 = (bf16[1,1,128,4096]{3,2,1,0:T(8,128)(2,1)}, bf16[1,1,128,4096]{3,2,1,0:T(8,128)(2,1)S(1)}, u32[]{:S(2)}, u32[]{:S(2)}) collective-permute-start(bf16[1,1,128,4096]{3,2,1,0:T(8,128)(2,1)} %param.8), channel_id=1, source_target_pairs={{12,0},{24,12},{36,24},{60,48},{72,60},{84,72},{108,96},{120,108},... | collective-permute-start | bytes 3145736 | tf_op jit(solution)/shard_map/ppermute | solution.py:60
  3.1 1.2 copy-done
  4.3 1.2 copy-done.1
  5.5 1.1 cut.1
  6.6 1.4 collective-permute-start.9
  8.0 1.4 collective-permute-start.11
  9.3 2.9 %collective-permute-start.7 = (bf16[1,1,128,3072]{3,2,1,0:T(8,128)(2,1)}, bf16[1,1,128,3072]{3,2,1,0:T(8,128)(2,1)S(1)}, u32[]{:S(2)}, u32[]{:S(2)}) collective-permute-start(bf16[1,1,128,3072]{3,2,1,0:T(8,128)(2,1)} %bitcast.11), channel_id=1, source_target_pairs={{0,384},{12,396},{24,408},{36,420},{48,432},{60,444},{72,456},{84,... | collective-permute-start | bytes 2359304 | tf_op jit(solution)/shard_map/ppermute | solution.py:60
  12.3 0.7 collective-permute-start.8
  12.9 0.0 collective-permute-done.9
  13.0 6.8 %collective-permute-start = (bf16[1,1,128,1024]{3,2,1,0:T(8,128)(2,1)S(1)}, bf16[1,1,128,1024]{3,2,1,0:T(8,128)(2,1)S(1)}, u32[]{:S(2)}, u32[]{:S(2)}) collective-permute-start(bf16[1,1,128,1024]{3,2,1,0:T(8,128)(2,1)S(1)} %copy-done.2), channel_id=1, source_target_pairs={{0,384},{12,396},{24,408},{36,420},{48,432},{60,444},{72,456},{84,... | collective-permute-start | bytes 786440 | tf_op jit(solution)/shard_map/ppermute | solution.py:60
  19.8 0.0 collective-permute-done.11
  19.8 1.4 collective-permute-start.5
  21.2 0.0 collective-permute-done.8
  21.2 1.3 collective-permute-start.3
  22.5 40.0 %collective-permute-done = bf16[1,1,128,1024]{3,2,1,0:T(8,128)(2,1)S(1)} collective-permute-done((bf16[1,1,128,1024]{3,2,1,0:T(8,128)(2,1)S(1)}, bf16[1,1,128,1024]{3,2,1,0:T(8,128)(2,1)S(1)}, u32[]{:S(2)}, u32[]{:S(2)}) %collective-permute-start) | collective-permute-done | bytes 262176 | tf_op jit(solution)/shard_map/ppermute | solution.py:60
  62.4 0.7 collective-permute-start.10
  63.1 0.7 collective-permute-start.12
  65.2 0.1 add_convert_fusion
  65.3 0.1 add_convert_fusion.1
  65.4 0.7 copy-done.3
  66.0 0.1 pad.2.clone
  66.1 0.0 collective-permute-done.3
  66.1 2.9 %collective-permute-start.1 = (bf16[1,1,128,1024]{3,2,1,0:T(8,128)(2,1)S(1)}, bf16[1,1,128,1024]{3,2,1,0:T(8,128)(2,1)S(1)}, u32[]{:S(2)}, u32[]{:S(2)}) collective-permute-start(bf16[1,1,128,1024]{3,2,1,0:T(8,128)(2,1)S(1)} %bitcast.40), channel_id=1, source_target_pairs={{0,384},{1,385},{2,386},{3,387},{4,388},{5,389},{6,390},{7,391},{8... | collective-permute-start | bytes 786440 | tf_op jit(solution)/shard_map/ppermute | solution.py:52
  69.0 0.7 collective-permute-start.6
  69.7 0.0 collective-permute-done.12
  69.7 40.1 %collective-permute-start.4 = (bf16[1,1,128,1024]{3,2,1,0:T(8,128)(2,1)}, bf16[1,1,128,1024]{3,2,1,0:T(8,128)(2,1)S(1)}, u32[]{:S(2)}, u32[]{:S(2)}) collective-permute-start(bf16[1,1,128,1024]{3,2,1,0:T(8,128)(2,1)} %collective-permute-done.3), channel_id=1, source_target_pairs={{24,756},{72,36},{120,84},{168,132},{216,180},{264,228},{312,276},... | collective-permute-start | bytes 786440 | tf_op jit(solution)/shard_map/ppermute | solution.py:60
  109.8 0.1 maximum_maximum_fusion
  109.9 22.9 %all_to_all.11 = f32[12,1,12]{2,1,0:T(1,128)S(1)} all-to-all(f32[12,1,12]{2,1,0:T(1,128)S(1)} %all_to_all.7), channel_id=1, replica_groups=mesh['section'=64,'dp'=12] {'dp'}, dimensions={0} | all-to-all | bytes 1152 | tf_op jit(solution)/shard_map/all_to_all | solution.py:230
  132.7 0.0 collective-permute-done.2
  132.7 3.1 %shard_map.77 = (bf16[128,4096]{1,0:T(8,128)(2,1)}, bf16[128,1024]{1,0:T(8,128)(2,1)}) custom-call(f32[12,12]{1,0:T(8,128)S(1)} %bitcast.37, bf16[128,1024]{1,0:T(8,128)(2,1)S(1)} %bitcast.28, bf16[128,3072]{1,0:T(8,128)(2,1)S(1)} %bitcast.30, bf16[128,4096]{1,0:T(8,128)(2,1)S(1)} %bitcast.24, bf16[128,1024]{1,0:T(8,128)(2,1)S(1)} %bitcast.31, ...), custom_call_target="tpu_custom_call" | custom-call | flops 503316480 | bytes 2359296 | tf_op jit(solution)/shard_map/pallas_call | solution.py:156
  135.8 0.0 collective-permute-done.4
  135.9 1.7 %shard_map.78 = (bf16[128,4096]{1,0:T(8,128)(2,1)}, bf16[128,1024]{1,0:T(8,128)(2,1)}) custom-call(f32[12,12]{1,0:T(8,128)S(1)} %bitcast.38, bf16[128,1024]{1,0:T(8,128)(2,1)S(1)} %bitcast.29, bf16[128,1024]{1,0:T(8,128)(2,1)S(1)} %bitcast.34, bf16[128,4096]{1,0:T(8,128)(2,1)S(1)} %bitcast.25, ...), custom_call_target="tpu_custom_call", output_to_operand_aliasing={{0}: (6, {}), {1}: (7, {})} | custom-call | flops 167772160 | bytes 786432 | tf_op jit(solution)/shard_map/pallas_call | solution.py:156
  (14 shorter events, 0.0 us)
Async XLA Ops:
  0.6 132.1 %collective-permute-start.2 = (bf16[1,1,128,4096]{3,2,1,0:T(8,128)(2,1)}, bf16[1,1,128,4096]{3,2,1,0:T(8,128)(2,1)S(1)}, u32[]{:S(2)}, u32[]{:S(2)}) collective-permute-start(bf16[1,1,128,4096]{3,2,1,0:T(8,128)(2,1)} %param.8), channel_id=1, source_target_pairs={{12,0},{24,12},{36,24},{60,48},{72,60},{84,72},{108,96},{120,108},... | collective-permute-start | bytes 3145736 | tf_op jit(solution)/shard_map/ppermute | solution.py:60
  3.1 1.2 copy-start
  4.3 1.2 copy-start.1
  5.5 7.4 %copy-start.2 = (bf16[1,1,128,1024]{3,2,1,0:T(8,128)(2,1)S(1)}, bf16[1,1,128,1024]{3,2,1,0:T(8,128)(2,1)}, u32[]{:S(2)}) copy-start(bf16[1,1,128,1024]{3,2,1,0:T(8,128)(2,1)} %param.7) | copy-start | bytes 786436
  6.6 6.3 %collective-permute-start.9 = (bf16[1,1,128,1024]{3,2,1,0:T(8,128)(2,1)S(1)}, bf16[1,1,128,1024]{3,2,1,0:T(8,128)(2,1)}, u32[]{:S(2)}, u32[]{:S(2)}) collective-permute-start(bf16[1,1,128,1024]{3,2,1,0:T(8,128)(2,1)S(1)} %bitcast.44), channel_id=1, source_target_pairs={{0,36},{48,84},{96,132},{144,180},{192,228},{240,276},{288,324},{3... | collective-permute-start | bytes 786440 | tf_op jit(solution)/shard_map/ppermute | solution.py:60
  8.0 11.8 %collective-permute-start.11 = (bf16[1,1,128,1024]{3,2,1,0:T(8,128)(2,1)S(1)}, bf16[1,1,128,1024]{3,2,1,0:T(8,128)(2,1)}, u32[]{:S(2)}, u32[]{:S(2)}) collective-permute-start(bf16[1,1,128,1024]{3,2,1,0:T(8,128)(2,1)S(1)} %bitcast.43), channel_id=1, source_target_pairs={{0,12},{48,60},{96,108},{144,156},{192,204},{240,252},{288,300},{3... | collective-permute-start | bytes 786440 | tf_op jit(solution)/shard_map/ppermute | solution.py:60
  9.3 123.4 %collective-permute-start.7 = (bf16[1,1,128,3072]{3,2,1,0:T(8,128)(2,1)}, bf16[1,1,128,3072]{3,2,1,0:T(8,128)(2,1)S(1)}, u32[]{:S(2)}, u32[]{:S(2)}) collective-permute-start(bf16[1,1,128,3072]{3,2,1,0:T(8,128)(2,1)} %bitcast.11), channel_id=1, source_target_pairs={{0,384},{12,396},{24,408},{36,420},{48,432},{60,444},{72,456},{84,... | collective-permute-start | bytes 2359304 | tf_op jit(solution)/shard_map/ppermute | solution.py:60
  12.3 8.9 %collective-permute-start.8 = (bf16[1,1,128,1024]{3,2,1,0:T(8,128)(2,1)S(1)}, bf16[1,1,128,1024]{3,2,1,0:T(8,128)(2,1)S(1)}, u32[]{:S(2)}, u32[]{:S(2)}) collective-permute-start(bf16[1,1,128,1024]{3,2,1,0:T(8,128)(2,1)S(1)} %bitcast.42), channel_id=1, source_target_pairs={{0,756},{48,36},{96,84},{144,132},{192,180},{240,228},{288,276},{3... | collective-permute-start | bytes 786440 | tf_op jit(solution)/shard_map/ppermute | solution.py:60
  13.0 49.5 %collective-permute-start = (bf16[1,1,128,1024]{3,2,1,0:T(8,128)(2,1)S(1)}, bf16[1,1,128,1024]{3,2,1,0:T(8,128)(2,1)S(1)}, u32[]{:S(2)}, u32[]{:S(2)}) collective-permute-start(bf16[1,1,128,1024]{3,2,1,0:T(8,128)(2,1)S(1)} %copy-done.2), channel_id=1, source_target_pairs={{0,384},{12,396},{24,408},{36,420},{48,432},{60,444},{72,456},{84,... | collective-permute-start | bytes 786440 | tf_op jit(solution)/shard_map/ppermute | solution.py:60
  19.8 43.3 %collective-permute-start.5 = (bf16[1,1,128,1024]{3,2,1,0:T(8,128)(2,1)S(1)}, bf16[1,1,128,1024]{3,2,1,0:T(8,128)(2,1)}, u32[]{:S(2)}, u32[]{:S(2)}) collective-permute-start(bf16[1,1,128,1024]{3,2,1,0:T(8,128)(2,1)S(1)} %bitcast.39), channel_id=1, source_target_pairs={{144,242},{146,240},{148,246},{150,244},{152,250},{154,248},{156,2... | collective-permute-start | bytes 786440 | tf_op jit(solution)/shard_map/ppermute | solution.py:52
  21.2 44.9 %collective-permute-start.3 = (bf16[1,1,128,1024]{3,2,1,0:T(8,128)(2,1)S(1)}, bf16[1,1,128,1024]{3,2,1,0:T(8,128)(2,1)}, u32[]{:S(2)}, u32[]{:S(2)}) collective-permute-start(bf16[1,1,128,1024]{3,2,1,0:T(8,128)(2,1)S(1)} %bitcast.41), channel_id=1, source_target_pairs={{0,24},{48,72},{96,120},{144,168},{192,216},{240,264},{288,312},{3... | collective-permute-start | bytes 786440 | tf_op jit(solution)/shard_map/ppermute | solution.py:60
  62.4 6.6 %collective-permute-start.10 = (bf16[1,1,128,1024]{3,2,1,0:T(8,128)(2,1)}, bf16[1,1,128,1024]{3,2,1,0:T(8,128)(2,1)S(1)}, u32[]{:S(2)}, u32[]{:S(2)}) collective-permute-start(bf16[1,1,128,1024]{3,2,1,0:T(8,128)(2,1)} %collective-permute-done.9), channel_id=1, source_target_pairs={{36,756},{84,36},{132,84},{180,132},{228,180},{276,228},{324,276},... | collective-permute-start | bytes 786440 | tf_op jit(solution)/shard_map/ppermute | solution.py:60
  63.1 6.6 %collective-permute-start.12 = (bf16[1,1,128,1024]{3,2,1,0:T(8,128)(2,1)}, bf16[1,1,128,1024]{3,2,1,0:T(8,128)(2,1)S(1)}, u32[]{:S(2)}, u32[]{:S(2)}) collective-permute-start(bf16[1,1,128,1024]{3,2,1,0:T(8,128)(2,1)} %collective-permute-done.11), channel_id=1, source_target_pairs={{12,756},{60,36},{108,84},{156,132},{204,180},{252,228},{300,276},... | collective-permute-start | bytes 786440 | tf_op jit(solution)/shard_map/ppermute | solution.py:60
  65.3 0.7 copy-start.3
  66.1 69.7 %collective-permute-start.1 = (bf16[1,1,128,1024]{3,2,1,0:T(8,128)(2,1)S(1)}, bf16[1,1,128,1024]{3,2,1,0:T(8,128)(2,1)S(1)}, u32[]{:S(2)}, u32[]{:S(2)}) collective-permute-start(bf16[1,1,128,1024]{3,2,1,0:T(8,128)(2,1)S(1)} %bitcast.40), channel_id=1, source_target_pairs={{0,384},{1,385},{2,386},{3,387},{4,388},{5,389},{6,390},{7,391},{8... | collective-permute-start | bytes 786440 | tf_op jit(solution)/shard_map/ppermute | solution.py:52
  69.0 66.8 %collective-permute-start.6 = (bf16[1,1,128,1024]{3,2,1,0:T(8,128)(2,1)}, bf16[1,1,128,1024]{3,2,1,0:T(8,128)(2,1)S(1)}, u32[]{:S(2)}, u32[]{:S(2)}) collective-permute-start(bf16[1,1,128,1024]{3,2,1,0:T(8,128)(2,1)} %collective-permute-done.5), channel_id=1, source_target_pairs={{240,530},{242,528},{244,534},{246,532},{248,538},{250,536},{252,5... | collective-permute-start | bytes 786440 | tf_op jit(solution)/shard_map/ppermute | solution.py:52
  69.7 66.1 %collective-permute-start.4 = (bf16[1,1,128,1024]{3,2,1,0:T(8,128)(2,1)}, bf16[1,1,128,1024]{3,2,1,0:T(8,128)(2,1)S(1)}, u32[]{:S(2)}, u32[]{:S(2)}) collective-permute-start(bf16[1,1,128,1024]{3,2,1,0:T(8,128)(2,1)} %collective-permute-done.3), channel_id=1, source_target_pairs={{24,756},{72,36},{120,84},{168,132},{216,180},{264,228},{312,276},... | collective-permute-start | bytes 786440 | tf_op jit(solution)/shard_map/ppermute | solution.py:60
